TPU v7x, 32 devices: a whole 2x2x4 slice. The times are simulated.
32 devices in a mesh: gx: 4 (over x, core), gy: 4 (over z), gz: 2 (over y).
Axes of the slice: x: 2, y: 2, z: 4, core: 2. Of those that a mesh axis runs over, the one named last changes fastest.
Arguments:
- fine_coef: bfloat16 [256, 512], P(('gx', 'gy', 'gz')), may hold values from -6 to 6
- mid_leaf: bfloat16 [32, 512], P(('gx', 'gy', 'gz')), may hold values from -6 to 6
- mid_child: int32 [32, 8], P(('gx', 'gy', 'gz')), may hold values from 0 to 7, as said below
- mid_parent: int32 [32], P(('gx', 'gy', 'gz')), may hold values from 0 to 31, each once
- mid_refined: int32 [32], P(('gx', 'gy', 'gz')), may hold values 0 or 1
- fine_nbr: int32 [256, 27], P(('gx', 'gy', 'gz')), may hold values from -1 to 255, as said below
- mid_nbr: int32 [32, 27], P(('gx', 'gy', 'gz')), may hold values from -1 to 31, as said below
- coarse_nbr: int32 [4, 27], replicated, may hold values from -1 to 3, as said below
- op_factor: float32 [3, 32, 3, 8, 8], replicated, may hold values from -1 to 1
- term_weight: float32 [32], replicated, may hold values from 0.05 to 1
Outputs:
- fine_out: float32 [256, 512], P(('gx', 'gy', 'gz'))
- mid_out: float32 [32, 512], P(('gx', 'gy', 'gz'))
Inputs may be any that keep to these rules, and one draw needn't show every extreme that they name: `fine_nbr`: column d names the fine box adjacent across displacement (d // 9 - 1, d // 3 % 3 - 1, d % 3 - 1), or -1. Column 13 is the row's own box. Box g lies on device g // 8; the named box's device differs from the row's device along each of gx, gy, gz by 0 or by that component of the displacement. `mid_nbr`: column d names the middle box adjacent across displacement (d // 9 - 1, d // 3 % 3 - 1, d % 3 - 1), or -1. Column 13 is the row's own box. Box g lies on device g; the named box's device differs from the row's device along each of gx, gy, gz by 0 or by that component of the displacement. `coarse_nbr`: column d names the coarse box adjacent across displacement (d // 9 - 1, d // 3 % 3 - 1, d % 3 - 1), or -1. Column 13 is the row's own box. `mid_child`: the 1 row of one device together name each of its 8 local fine slots exactly once. `mid_parent`: each value appears once.
All inputs are finite; a program needn't handle non-finite values. No bound on the sum of `mid_refined` on one device may be relied on, other than what follows from the above.
Results may differ from a plain program's by a relative error of at most 0.006.
Values may be sent and summed in bfloat16 or wider, within the bound.
A program may use at most 64 MiB of HBM per device.

v0:
```python
import math

import jax
import jax.numpy as jnp
import numpy as np
from jax import lax
from jax.sharding import PartitionSpec as P

exact_mode = lax.Precision.HIGHEST


def padded_2(cells, sides, width):
    for axis, dim in sides:
        count = lax.axis_size(axis)
        ends = count - 1
        head = lax.slice_in_dim(cells, 0, width, axis=dim)
        tail = lax.slice_in_dim(cells, cells.shape[dim] - width, cells.shape[dim], axis=dim)
        cells = jnp.concatenate(
            [
                lax.ppermute(tail, axis, [(i, (i + 1) % count) for i in range(ends)]),
                cells,
                lax.ppermute(head, axis, [((i + 1) % count, i) for i in range(ends)]),
            ],
            axis=dim,
        )
    return cells


def poly_multiply(left, right):
    result = [0.0] * (len(left) + len(right) - 1)
    for first, left_coef in enumerate(left):
        for second, right_coef in enumerate(right):
            result[first + second] += left_coef * right_coef
    return result


def poly_compose(coeffs, factor, offset):
    result = [0.0]
    power_term = [1.0]
    for coef in coeffs:
        padded = result + [0.0] * (len(power_term) - len(result))
        result = [padded[place] + coef * power_term[place] for place in range(len(power_term))]
        power_term = poly_multiply(power_term, [offset, factor])
    return result


def legendre_table(basis_order):
    polys = [[1.0], [0.0, 1.0]]
    for degree in range(1, basis_order):
        upper = [0.0] + [(2 * degree + 1) * coef for coef in polys[degree]]
        lower = [degree * coef for coef in polys[degree - 1]] + [0.0] * (
            len(upper) - len(polys[degree - 1])
        )
        polys.append([(upper[place] - lower[place]) / (degree + 1) for place in range(len(upper))])
    return [
        [math.sqrt(2 * degree + 1) * coef for coef in poly_compose(polys[degree], 2.0, -1.0)]
        for degree in range(basis_order)
    ]


def two_scale(basis_order):
    shifted = legendre_table(basis_order)
    filters = np.zeros((2, basis_order, basis_order))
    for which_half in range(2):
        for row_at in range(basis_order):
            halved = poly_compose(shifted[row_at], 0.5, 0.5 * which_half)
            for col_at in range(basis_order):
                product = poly_multiply(halved, shifted[col_at])
                total = sum((coef / (place + 1) for place, coef in enumerate(product)))
                filters[which_half, row_at, col_at] = total / math.sqrt(2.0)
    return jnp.asarray(filters, jnp.float32)


def compress(children, filters):
    box_count = children.shape[0]
    basis_order = filters.shape[1]
    cube_form = children.reshape(box_count, 2, 2, 2, basis_order, basis_order, basis_order)
    section_one = jnp.einsum("bijlxyz,ipx->bjlpyz", cube_form, filters, precision=exact_mode)
    section_two = jnp.einsum("bjlpyz,jqy->blpqz", section_one, filters, precision=exact_mode)
    section_three = jnp.einsum("blpqz,lrz->bpqr", section_two, filters, precision=exact_mode)
    return section_three.reshape(box_count, basis_order**3)


def prolong(parents, filters):
    box_count = parents.shape[0]
    basis_order = filters.shape[1]
    cube_form = parents.reshape(box_count, basis_order, basis_order, basis_order)
    section_one = jnp.einsum("bpqr,ipx->bixqr", cube_form, filters, precision=exact_mode)
    section_two = jnp.einsum("bixqr,jqy->bijxyr", section_one, filters, precision=exact_mode)
    section_three = jnp.einsum("bijxyr,lrz->bijlxyz", section_two, filters, precision=exact_mode)
    return section_three.reshape(box_count, 8, basis_order**3)


def level_tables(factors, weights):
    basis_order = factors.shape[-1]
    term_count = factors.shape[0]
    plane_size = basis_order * basis_order
    row_total = term_count * plane_size
    row_id = jnp.arange(row_total, dtype=jnp.int32)
    term_of = row_id // plane_size
    first_of = row_id // basis_order % basis_order
    second_of = row_id % basis_order
    pair_id = jnp.arange(term_count * basis_order, dtype=jnp.int32)
    select_first = ((term_of * basis_order + first_of)[:, None] == pair_id[None, :]).astype(
        jnp.float32
    )
    select_second = ((term_of * basis_order + second_of)[:, None] == pair_id[None, :]).astype(
        jnp.float32
    )
    col_id = jnp.arange(plane_size, dtype=jnp.int32)
    order_id = jnp.arange(basis_order, dtype=jnp.int32)
    spread_outer = (order_id[:, None] == (col_id // basis_order)[None, :]).astype(jnp.float32)
    spread_inner = (order_id[:, None] == (col_id % basis_order)[None, :]).astype(jnp.float32)
    across = jnp.transpose(factors, (1, 0, 3, 2)).reshape(3, term_count * basis_order, basis_order)
    left_pick = jnp.einsum("rs,esb->erb", select_first, across, precision=exact_mode)
    left_full = jnp.einsum("erb,bq->erq", left_pick, spread_outer, precision=exact_mode)
    right_pick = jnp.einsum("rs,esc->erc", select_second, across, precision=exact_mode)
    right_full = jnp.einsum("erc,cq->erq", right_pick, spread_inner, precision=exact_mode)
    weight_rows = jnp.dot(select_first, jnp.repeat(weights, basis_order), precision=exact_mode)
    blocks = weight_rows[None, None, :, None] * left_full[:, None] * right_full[None, :]
    return (factors.astype(jnp.bfloat16), blocks.astype(jnp.bfloat16))


def apply_boxes(sources, factor_bf, blocks):
    box_count = sources.shape[0]
    basis_order = factor_bf.shape[-1]
    plane_size = basis_order * basis_order
    cube_form = sources.reshape(box_count, 3, 3, 3, basis_order, plane_size)
    running = jnp.zeros((box_count * basis_order, plane_size), jnp.float32)
    for along_y in range(3):
        for along_z in range(3):
            picked = cube_form[:, :, along_y, along_z]
            mixed_terms = jnp.einsum(
                "mdax,bdxq->bamq", factor_bf, picked, preferred_element_type=jnp.float32
            ).astype(jnp.bfloat16)
            flat_terms = mixed_terms.reshape(box_count * basis_order, -1)
            running = running + jnp.dot(
                flat_terms, blocks[along_y, along_z], preferred_element_type=jnp.float32
            )
    return running.reshape(box_count, basis_order**3)


def pick_sources(source_table, near_ids):
    return source_table[jnp.maximum(near_ids, 0)] * (near_ids >= 0)[:, :, None].astype(jnp.bfloat16)


def apply_picked(source_table, near_ids, factor_bf, blocks):
    total_rows = near_ids.shape[0]
    group_rows = math.gcd(total_rows, 16)
    grouped = near_ids.reshape(total_rows // group_rows, group_rows, 27)

    def one_group(some_rows):
        return apply_boxes(pick_sources(source_table, some_rows), factor_bf, blocks)

    return lax.map(one_group, grouped).reshape(total_rows, -1)


def local_rows(near_ids, per_device):
    size_y = lax.axis_size("gy")
    size_z = lax.axis_size("gz")
    mine_x = lax.axis_index("gx")
    mine_y = lax.axis_index("gy")
    mine_z = lax.axis_index("gz")
    device = near_ids // per_device
    slot_at = near_ids % per_device
    other_x = device // (size_y * size_z)
    other_y = device // size_z % size_y
    other_z = device % size_z
    cell_at = (other_x - mine_x + 1) * 9 + (other_y - mine_y + 1) * 3 + (other_z - mine_z + 1)
    return jnp.where(near_ids >= 0, cell_at * per_device + slot_at, -1)


def near_fine(detail):
    shaped = detail.reshape((1, 1, 1) + detail.shape)
    extended = padded_2(shaped, (("gx", 0), ("gy", 1), ("gz", 2)), 1)
    return extended.reshape(-1, detail.shape[1])


def near_mid(detail):
    shaped = detail.reshape((1, 1, 1) + detail.shape)
    extended = padded_2(shaped, (("gx", 0), ("gy", 1), ("gz", 2)), 1)
    return extended.reshape(-1, detail.shape[1])


def shards(
    fine_coef,
    mid_leaf,
    mid_child,
    mid_parent,
    mid_refined,
    fine_nbr,
    mid_nbr,
    coarse_nbr,
    op_factor,
    term_weight,
):
    basis_order = op_factor.shape[-1]
    filters = two_scale(basis_order)
    mid_local = mid_child.shape[0]
    slots_dev = fine_coef.shape[0]
    coarse_count = coarse_nbr.shape[0]
    child_hot = (
        mid_child[:, :, None] == jnp.arange(slots_dev, dtype=jnp.int32)[None, None, :]
    ).astype(jnp.float32)
    refined = mid_refined.astype(jnp.float32)
    live_mask = jnp.einsum("mos,m->s", child_hot, refined, precision=exact_mode)
    children = fine_coef[mid_child].astype(jnp.float32)
    compressed = compress(children, filters)
    mid_source = jnp.where(
        mid_refined[:, None] > 0, compressed, mid_leaf.astype(jnp.float32)
    ).astype(jnp.bfloat16)
    mid_float = mid_source.astype(jnp.float32)
    spread = prolong(mid_float, filters)
    fine_from = jnp.einsum("mos,mok->sk", child_hot, spread, precision=exact_mode)
    fine_detail = (live_mask[:, None] * (fine_coef.astype(jnp.float32) - fine_from)).astype(
        jnp.bfloat16
    )
    parent = mid_parent // 8
    octant = mid_parent % 8
    octant_hot = (octant[:, None] == jnp.arange(8, dtype=jnp.int32)[None, :]).astype(jnp.float32)
    parent_hot = (parent[:, None] == jnp.arange(coarse_count, dtype=jnp.int32)[None, :]).astype(
        jnp.float32
    )
    placed = octant_hot[:, :, None] * mid_float[:, None, :]
    contribution = compress(placed, filters)
    partial_sum = jnp.dot(parent_hot.T, contribution, precision=exact_mode)
    coarse_source = lax.psum(partial_sum, ("gx", "gy", "gz"))
    fine_table = near_fine(fine_detail)
    fine_factor, fine_blocks = level_tables(op_factor[0], term_weight)
    fine_direct = apply_picked(
        fine_table, local_rows(fine_nbr, slots_dev), fine_factor, fine_blocks
    )
    parent_source = jnp.dot(parent_hot, coarse_source, precision=exact_mode)
    from_coarse = jnp.einsum(
        "mo,mok->mk", octant_hot, prolong(parent_source, filters), precision=exact_mode
    )
    mid_detail = (mid_float - from_coarse).astype(jnp.bfloat16)
    mid_table = near_mid(mid_detail)
    mid_factor, mid_blocks = level_tables(op_factor[1], term_weight)
    mid_direct = apply_picked(mid_table, local_rows(mid_nbr, mid_local), mid_factor, mid_blocks)
    coarse_table = coarse_source.astype(jnp.bfloat16)
    coarse_factor, coarse_blocks = level_tables(op_factor[2], term_weight)
    parent_out = apply_picked(coarse_table, coarse_nbr[parent], coarse_factor, coarse_blocks)
    mid_out = mid_direct + jnp.einsum(
        "mo,mok->mk", octant_hot, prolong(parent_out, filters), precision=exact_mode
    )
    fine_back = jnp.einsum(
        "mos,mok->sk", child_hot, prolong(mid_out, filters), precision=exact_mode
    )
    fine_out = live_mask[:, None] * (fine_direct + fine_back)
    return (fine_out, mid_out)


def solution(mesh):
    return jax.shard_map(
        shards,
        mesh=mesh,
        in_specs=(
            P(("gx", "gy", "gz"), None),
            P(("gx", "gy", "gz"), None),
            P(("gx", "gy", "gz"), None),
            P(("gx", "gy", "gz")),
            P(("gx", "gy", "gz")),
            P(("gx", "gy", "gz"), None),
            P(("gx", "gy", "gz"), None),
            P(),
            P(),
            P(),
        ),
        out_specs=(P(("gx", "gy", "gz"), None), P(("gx", "gy", "gz"), None)),
        check_vma=False,
    )
```

profile of v0, /device:TPU:10, one launch (start us, length us, event | category | flops | bytes accessed | tf_op | source)
XLA Modules:
  0.0 179.6 jit_solution(12119286320038687831)
XLA Ops:
  2.7 1.3 gather_fusion
  11.1 41.2 %psum.7 = f32[4,512]{1,0:T(4,128)S(1)} all-reduce(f32[4,512]{1,0:T(4,128)S(1)} %broadcast_multiply_fusion), channel_id=1, replica_groups=mesh['gx'=4,'gy'=4,'gz'=2] {'gx','gy','gz'}, use_global_device_ids=true, to_apply=%region_1.2 | all-reduce | flops 2048 | bytes 16384 | tf_op jit(solution)/shard_map/psum | solution.py:227
  54.7 2.6 %convolution_bitcast_fusion.17 = f32[1,2,2,2,8,8,8]{5,6,4,2,1,3,0:T(8,128)S(1)} fusion(f32[2,8,8,1,1,1]{2,1,5,4,3,0:T(8,128)} %constant.328, f32[2,2,8,8,8]{4,3,2,0,1:T(8,128)S(1)} %convolution_bitcast_fusion.41), kind=kOutput, calls=%fused_computation.48 | convolution fusion | flops 393216 | bytes 25088 | tf_op jit(solution)/shard_map/bijxyr,lrz->bijlxyz/dot_general | solution.py:90
  57.7 1.9 %collective-permute-start.6 = (bf16[1,1,1,1,512]{4,2,1,0,3:T(2,128)(2,1)S(1)}, bf16[1,1,1,1,512]{4,2,1,0,3:T(2,128)(2,1)S(1)}, u32[]{:S(2)}, u32[]{:S(2)}) collective-permute-start(bf16[1,1,1,1,512]{4,2,1,0,3:T(2,128)(2,1)S(1)} %fusion.60), channel_id=1, source_target_pairs={{0,8},{8,16},{16,24},{1,9},{9,17},{17,25},{2,10},{10,18},{18,26},{... | collective-permute-start | bytes 3080 | tf_op jit(solution)/shard_map/ppermute | solution.py:20
  59.6 3.6 %collective-permute-start.7 = (bf16[1,1,1,1,512]{4,2,1,0,3:T(2,128)(2,1)S(1)}, bf16[1,1,1,1,512]{4,2,1,0,3:T(2,128)(2,1)S(1)}, u32[]{:S(2)}, u32[]{:S(2)}) collective-permute-start(bf16[1,1,1,1,512]{4,2,1,0,3:T(2,128)(2,1)S(1)} %fusion.60), channel_id=1, source_target_pairs={{8,0},{16,8},{24,16},{9,1},{17,9},{25,17},{10,2},{18,10},{26,18},{... | collective-permute-start | bytes 3080 | tf_op jit(solution)/shard_map/ppermute | solution.py:22
  64.1 1.9 %convolution_bitcast_fusion.18 = f32[1,2,2,2,8,8,8]{5,6,4,2,1,3,0:T(8,128)S(1)} fusion(f32[2,8,8,1,1,1]{2,1,5,4,3,0:T(8,128)S(1)} %copy-done.6, f32[2,2,8,8,8]{4,3,2,0,1:T(8,128)S(1)} %convolution_bitcast_fusion.42), kind=kOutput, calls=%fused_computation.49 | convolution fusion | flops 393216 | bytes 25088 | tf_op jit(solution)/shard_map/bijxyr,lrz->bijlxyz/dot_general | solution.py:90
  66.5 1.9 %collective-permute-start = (bf16[1,1,1,8,512]{4,3,2,1,0:T(8,128)(2,1)S(1)}, bf16[1,1,1,8,512]{4,3,2,1,0:T(8,128)(2,1)S(1)}, u32[]{:S(2)}, u32[]{:S(2)}) collective-permute-start(bf16[1,1,1,8,512]{4,3,2,1,0:T(8,128)(2,1)S(1)} %fusion.58), channel_id=1, source_target_pairs={{0,8},{8,16},{16,24},{1,9},{9,17},{17,25},{2,10},{10,18},{18,26},{... | collective-permute-start | bytes 24584 | tf_op jit(solution)/shard_map/ppermute | solution.py:20
  68.5 3.6 %collective-permute-start.1 = (bf16[1,1,1,8,512]{4,3,2,1,0:T(8,128)(2,1)S(1)}, bf16[1,1,1,8,512]{4,3,2,1,0:T(8,128)(2,1)S(1)}, u32[]{:S(2)}, u32[]{:S(2)}) collective-permute-start(bf16[1,1,1,8,512]{4,3,2,1,0:T(8,128)(2,1)S(1)} %fusion.58), channel_id=1, source_target_pairs={{8,0},{16,8},{24,16},{9,1},{17,9},{25,17},{10,2},{18,10},{26,18},{... | collective-permute-start | bytes 24584 | tf_op jit(solution)/shard_map/ppermute | solution.py:22
  75.8 1.5 convolution_bitcast_fusion.1
  77.2 1.3 convolution_bitcast_fusion
  78.9 1.3 convolution_bitcast_fusion.3
  80.2 1.3 convolution_bitcast_fusion.2
  81.9 1.3 convolution_bitcast_fusion.5
  83.2 1.3 convolution_bitcast_fusion.4
  91.4 1.9 %convolution_bitcast_fusion.16 = f32[1,2,2,2,8,8,8]{5,6,4,2,1,3,0:T(8,128)S(1)} fusion(f32[2,8,8,1,1,1]{2,1,5,4,3,0:T(8,128)S(1)} %copy-done.6, f32[2,2,8,8,8]{4,3,2,0,1:T(8,128)S(1)} %convolution_bitcast_fusion.40), kind=kOutput, calls=%fused_computation.47 | convolution fusion | flops 393216 | bytes 25088 | tf_op jit(solution)/shard_map/bijxyr,lrz->bijlxyz/dot_general | solution.py:90
  97.1 2.0 %multiply_convert_fusion.1 = bf16[3,3,2048,64]{2,3,1,0:T(8,128)(2,1)} fusion(f32[3,2048,64]{1,2,0:T(8,128)S(1)} %fusion.155, f32[3,2048,64]{1,2,0:T(8,128)S(1)} %convolution_multiply_fusion.1), kind=kLoop, calls=%fused_computation.5 | loop fusion | flops 2359296 | bytes 5505024 | tf_op jit(solution)/shard_map/convert_element_type | solution.py:121
  99.7 3.3 %collective-permute-start.8 = (bf16[3,1,1,1,512]{4,2,1,0,3:T(2,128)(2,1)S(1)}, bf16[3,1,1,1,512]{4,2,1,0,3:T(2,128)(2,1)S(1)}, u32[]{:S(2)}, u32[]{:S(2)}) collective-permute-start(bf16[3,1,1,1,512]{4,2,1,0,3:T(2,128)(2,1)S(1)} %pad_maximum_fusion.5), channel_id=1, source_target_pairs={{0,2},{2,4},{4,6},{1,3},{3,5},{5,7},{8,10},{10,12},{12,14},{9,11},... | collective-permute-start | bytes 9224 | tf_op jit(solution)/shard_map/ppermute | solution.py:20
  103.0 2.5 %collective-permute-start.9 = (bf16[3,1,1,1,512]{4,2,1,0,3:T(2,128)(2,1)S(1)}, bf16[3,1,1,1,512]{4,2,1,0,3:T(2,128)(2,1)S(1)}, u32[]{:S(2)}, u32[]{:S(2)}) collective-permute-start(bf16[3,1,1,1,512]{4,2,1,0,3:T(2,128)(2,1)S(1)} %pad_maximum_fusion.5), channel_id=1, source_target_pairs={{2,0},{4,2},{6,4},{3,1},{5,3},{7,5},{10,8},{12,10},{14,12},{11,9},... | collective-permute-start | bytes 9224 | tf_op jit(solution)/shard_map/ppermute | solution.py:22
  106.1 2.5 %collective-permute-done.9 = bf16[3,1,1,1,512]{4,2,1,0,3:T(2,128)(2,1)S(1)} collective-permute-done((bf16[3,1,1,1,512]{4,2,1,0,3:T(2,128)(2,1)S(1)}, bf16[3,1,1,1,512]{4,2,1,0,3:T(2,128)(2,1)S(1)}, u32[]{:S(2)}, u32[]{:S(2)}) %collective-permute-start.9) | collective-permute-done | bytes 3104 | tf_op jit(solution)/shard_map/ppermute | solution.py:22
  108.6 2.5 %collective-permute-start.10 = (bf16[3,3,1,1,512]{4,2,1,0,3:T(2,128)(2,1)S(1)}, bf16[3,3,1,1,512]{4,2,1,0,3:T(2,128)(2,1)S(1)}, u32[]{:S(2)}, u32[]{:S(2)}) collective-permute-start(bf16[3,3,1,1,512]{4,2,1,0,3:T(2,128)(2,1)S(1)} %pad_maximum_fusion.4), channel_id=1, source_target_pairs={{0,1},{2,3},{4,5},{6,7},{8,9},{10,11},{12,13},{14,15},{16,17},{18,... | collective-permute-start | bytes 27656 | tf_op jit(solution)/shard_map/ppermute | solution.py:20
  111.1 1.3 collective-permute-start.11
  112.4 2.3 %collective-permute-start.2 = (bf16[3,1,1,8,512]{4,3,2,1,0:T(8,128)(2,1)S(1)}, bf16[3,1,1,8,512]{4,3,2,1,0:T(8,128)(2,1)S(1)}, u32[]{:S(2)}, u32[]{:S(2)}) collective-permute-start(bf16[3,1,1,8,512]{4,3,2,1,0:T(8,128)(2,1)S(1)} %pad_maximum_fusion.3), channel_id=1, source_target_pairs={{0,2},{2,4},{4,6},{1,3},{3,5},{5,7},{8,10},{10,12},{12,14},{9,11},... | collective-permute-start | bytes 73736 | tf_op jit(solution)/shard_map/ppermute | solution.py:20
  114.7 3.7 %collective-permute-start.3 = (bf16[3,1,1,8,512]{4,3,2,1,0:T(8,128)(2,1)S(1)}, bf16[3,1,1,8,512]{4,3,2,1,0:T(8,128)(2,1)S(1)}, u32[]{:S(2)}, u32[]{:S(2)}) collective-permute-start(bf16[3,1,1,8,512]{4,3,2,1,0:T(8,128)(2,1)S(1)} %pad_maximum_fusion.3), channel_id=1, source_target_pairs={{2,0},{4,2},{6,4},{3,1},{5,3},{7,5},{10,8},{12,10},{14,12},{11,9},... | collective-permute-start | bytes 73736 | tf_op jit(solution)/shard_map/ppermute | solution.py:22
  123.7 1.1 convolution_add_fusion.24
  124.8 1.1 convolution_add_fusion.23
  125.9 1.1 convolution_add_fusion.22
  127.1 1.1 convolution_add_fusion.21
  133.6 4.5 %collective-permute-start.4 = (bf16[3,3,1,8,512]{4,3,2,1,0:T(8,128)(2,1)S(1)}, bf16[3,3,1,8,512]{4,3,2,1,0:T(8,128)(2,1)S(1)}, u32[]{:S(2)}, u32[]{:S(2)}) collective-permute-start(bf16[3,3,1,8,512]{4,3,2,1,0:T(8,128)(2,1)S(1)} %pad_maximum_fusion.1), channel_id=1, source_target_pairs={{0,1},{2,3},{4,5},{6,7},{8,9},{10,11},{12,13},{14,15},{16,17},{18,... | collective-permute-start | bytes 221192 | tf_op jit(solution)/shard_map/ppermute | solution.py:20
  138.1 1.3 collective-permute-start.5
  139.4 1.9 %convolution_bitcast_fusion.15 = f32[1,2,2,2,8,8,8]{5,6,4,2,1,3,0:T(8,128)S(1)} fusion(f32[2,8,8,1,1,1]{2,1,5,4,3,0:T(8,128)S(1)} %copy-done.6, f32[2,2,8,8,8]{4,3,2,0,1:T(8,128)S(1)} %convolution_bitcast_fusion.39), kind=kOutput, calls=%fused_computation.46 | convolution fusion | flops 393216 | bytes 25088 | tf_op jit(solution)/shard_map/bijxyr,lrz->bijlxyz/dot_general | solution.py:90
  141.6 2.8 %collective-permute-done.5 = bf16[3,3,1,8,512]{4,3,2,1,0:T(8,128)(2,1)S(1)} collective-permute-done((bf16[3,3,1,8,512]{4,3,2,1,0:T(8,128)(2,1)S(1)}, bf16[3,3,1,8,512]{4,3,2,1,0:T(8,128)(2,1)S(1)}, u32[]{:S(2)}, u32[]{:S(2)}) %collective-permute-start.5) | collective-permute-done | bytes 73760 | tf_op jit(solution)/shard_map/ppermute | solution.py:22
  146.0 1.1 fusion.18
  147.2 1.1 fusion.17
  150.6 1.2 fusion.14
  151.7 1.1 fusion.13
  154.7 2.2 %reshape.817 = bf16[64,2048]{1,0:T(8,128)(2,1)} reshape(bf16[8,8,32,64]{3,2,1,0:T(8,128)(2,1)} %fusion.18) | data formatting | bytes 524288 | tf_op jit(solution)/shard_map/while/body/eval_jaxpr/reshape | solution.py:136
  156.9 2.2 %reshape.820 = bf16[64,2048]{1,0:T(8,128)(2,1)} reshape(bf16[8,8,32,64]{3,2,1,0:T(8,128)(2,1)} %fusion.17) | data formatting | bytes 524288 | tf_op jit(solution)/shard_map/while/body/eval_jaxpr/reshape | solution.py:136
  159.1 2.2 %reshape.821 = bf16[64,2048]{1,0:T(8,128)(2,1)} reshape(bf16[8,8,32,64]{3,2,1,0:T(8,128)(2,1)} %fusion.16) | data formatting | bytes 524288 | tf_op jit(solution)/shard_map/while/body/eval_jaxpr/reshape | solution.py:136
  161.3 2.2 %reshape.822 = bf16[64,2048]{1,0:T(8,128)(2,1)} reshape(bf16[8,8,32,64]{3,2,1,0:T(8,128)(2,1)} %fusion.15) | data formatting | bytes 524288 | tf_op jit(solution)/shard_map/while/body/eval_jaxpr/reshape | solution.py:136
  163.5 2.2 %reshape.823 = bf16[64,2048]{1,0:T(8,128)(2,1)} reshape(bf16[8,8,32,64]{3,2,1,0:T(8,128)(2,1)} %fusion.14) | data formatting | bytes 524288 | tf_op jit(solution)/shard_map/while/body/eval_jaxpr/reshape | solution.py:136
  165.7 2.2 %reshape.824 = bf16[64,2048]{1,0:T(8,128)(2,1)} reshape(bf16[8,8,32,64]{3,2,1,0:T(8,128)(2,1)} %fusion.13) | data formatting | bytes 524288 | tf_op jit(solution)/shard_map/while/body/eval_jaxpr/reshape | solution.py:136
  168.0 2.2 %reshape.825 = bf16[64,2048]{1,0:T(8,128)(2,1)} reshape(bf16[8,8,32,64]{3,2,1,0:T(8,128)(2,1)} %fusion.12) | data formatting | bytes 524288 | tf_op jit(solution)/shard_map/while/body/eval_jaxpr/reshape | solution.py:136
  170.2 1.2 reshape.826
  171.8 1.2 fusion.70
  173.0 1.2 convolution_add_fusion.7
  174.2 1.2 convolution_add_fusion.6
  175.4 1.2 convolution_add_fusion.5
  176.5 1.2 convolution_add_fusion.4
  (203 shorter events, 46.6 us)
Async XLA Ops:
  0.6 62.9 %copy-start.5 = (f32[2,8,8,1]{2,1,3,0:T(8,128)S(1)}, f32[2,8,8,1]{2,1,3,0:T(8,128)}, u32[]{:S(2)}) copy-start(f32[2,8,8,1]{2,1,3,0:T(8,128)} %constant.330) | copy-start | bytes 1540
  0.6 63.1 %copy-start.7 = (f32[2,8,8,1,1]{2,1,4,3,0:T(8,128)S(1)}, f32[2,8,8,1,1]{2,1,4,3,0:T(8,128)}, u32[]{:S(2)}) copy-start(f32[2,8,8,1,1]{2,1,4,3,0:T(8,128)} %constant.329) | copy-start | bytes 1540
  0.7 63.4 %copy-start.6 = (f32[2,8,8,1,1,1]{2,1,5,4,3,0:T(8,128)S(1)}, f32[2,8,8,1,1,1]{2,1,5,4,3,0:T(8,128)}, u32[]{:S(2)}) copy-start(f32[2,8,8,1,1,1]{2,1,5,4,3,0:T(8,128)} %constant.328) | copy-start | bytes 1540
  0.7 62.6 %copy-start.13 = (s32[1,8]{1,0:T(1,128)S(1)}, s32[1,8]{1,0:T(1,128)}, u32[]{:S(2)}) copy-start(s32[1,8]{1,0:T(1,128)} %param.13) | copy-start | bytes 100
  4.0 62.3 %copy-start.4 = (bf16[8,512]{1,0:T(8,128)(2,1)S(1)}, bf16[8,512]{1,0:T(8,128)(2,1)}, u32[]{:S(2)}) copy-start(bf16[8,512]{1,0:T(8,128)(2,1)} %param.11) | copy-start | bytes 24580
  4.2 68.0 %copy-start.3 = (f32[3,32,3,8,8]{1,4,3,2,0:T(8,128)S(1)}, f32[3,32,3,8,8]{1,4,3,2,0:T(8,128)}, u32[]{:S(2)}) copy-start(f32[3,32,3,8,8]{1,4,3,2,0:T(8,128)} %param.19) | copy-start | bytes 221188
  9.0 63.3 %copy-start.12 = (s32[4,27]{1,0:T(4,128)S(1)}, s32[4,27]{1,0:T(4,128)}, u32[]{:S(2)}) copy-start(s32[4,27]{1,0:T(4,128)} %param.18) | copy-start | bytes 1300
  52.4 20.6 %copy-start.10 = (s32[1,27]{1,0:T(1,128)S(1)}, s32[1,27]{1,0:T(1,128)}, u32[]{:S(2)}) copy-start(s32[1,27]{1,0:T(1,128)} %param.17) | copy-start | bytes 328
  57.7 42.0 %collective-permute-start.6 = (bf16[1,1,1,1,512]{4,2,1,0,3:T(2,128)(2,1)S(1)}, bf16[1,1,1,1,512]{4,2,1,0,3:T(2,128)(2,1)S(1)}, u32[]{:S(2)}, u32[]{:S(2)}) collective-permute-start(bf16[1,1,1,1,512]{4,2,1,0,3:T(2,128)(2,1)S(1)} %fusion.60), channel_id=1, source_target_pairs={{0,8},{8,16},{16,24},{1,9},{9,17},{17,25},{2,10},{10,18},{18,26},{... | collective-permute-start | bytes 3080 | tf_op jit(solution)/shard_map/ppermute | solution.py:20
  59.6 40.1 %collective-permute-start.7 = (bf16[1,1,1,1,512]{4,2,1,0,3:T(2,128)(2,1)S(1)}, bf16[1,1,1,1,512]{4,2,1,0,3:T(2,128)(2,1)S(1)}, u32[]{:S(2)}, u32[]{:S(2)}) collective-permute-start(bf16[1,1,1,1,512]{4,2,1,0,3:T(2,128)(2,1)S(1)} %fusion.60), channel_id=1, source_target_pairs={{8,0},{16,8},{24,16},{9,1},{17,9},{25,17},{10,2},{18,10},{26,18},{... | collective-permute-start | bytes 3080 | tf_op jit(solution)/shard_map/ppermute | solution.py:22
  66.5 45.8 %collective-permute-start = (bf16[1,1,1,8,512]{4,3,2,1,0:T(8,128)(2,1)S(1)}, bf16[1,1,1,8,512]{4,3,2,1,0:T(8,128)(2,1)S(1)}, u32[]{:S(2)}, u32[]{:S(2)}) collective-permute-start(bf16[1,1,1,8,512]{4,3,2,1,0:T(8,128)(2,1)S(1)} %fusion.58), channel_id=1, source_target_pairs={{0,8},{8,16},{16,24},{1,9},{9,17},{17,25},{2,10},{10,18},{18,26},{... | collective-permute-start | bytes 24584 | tf_op jit(solution)/shard_map/ppermute | solution.py:20
  68.5 43.9 %collective-permute-start.1 = (bf16[1,1,1,8,512]{4,3,2,1,0:T(8,128)(2,1)S(1)}, bf16[1,1,1,8,512]{4,3,2,1,0:T(8,128)(2,1)S(1)}, u32[]{:S(2)}, u32[]{:S(2)}) collective-permute-start(bf16[1,1,1,8,512]{4,3,2,1,0:T(8,128)(2,1)S(1)} %fusion.58), channel_id=1, source_target_pairs={{8,0},{16,8},{24,16},{9,1},{17,9},{25,17},{10,2},{18,10},{26,18},{... | collective-permute-start | bytes 24584 | tf_op jit(solution)/shard_map/ppermute | solution.py:22
  77.2 7.4 %copy-start.11 = (f32[32]{0:T(128)S(1)}, f32[32]{0:T(128)}, u32[]{:S(2)}) copy-start(f32[32]{0:T(128)} %param.20) | copy-start | bytes 388
  91.4 4.0 %copy-start.9 = (s32[8,27]{1,0:T(8,128)S(1)}, s32[8,27]{1,0:T(8,128)}, u32[]{:S(2)}) copy-start(s32[8,27]{1,0:T(8,128)} %param.16) | copy-start | bytes 2596
  99.7 6.3 %collective-permute-start.8 = (bf16[3,1,1,1,512]{4,2,1,0,3:T(2,128)(2,1)S(1)}, bf16[3,1,1,1,512]{4,2,1,0,3:T(2,128)(2,1)S(1)}, u32[]{:S(2)}, u32[]{:S(2)}) collective-permute-start(bf16[3,1,1,1,512]{4,2,1,0,3:T(2,128)(2,1)S(1)} %pad_maximum_fusion.5), channel_id=1, source_target_pairs={{0,2},{2,4},{4,6},{1,3},{3,5},{5,7},{8,10},{10,12},{12,14},{9,11},... | collective-permute-start | bytes 9224 | tf_op jit(solution)/shard_map/ppermute | solution.py:20
  103.0 5.5 %collective-permute-start.9 = (bf16[3,1,1,1,512]{4,2,1,0,3:T(2,128)(2,1)S(1)}, bf16[3,1,1,1,512]{4,2,1,0,3:T(2,128)(2,1)S(1)}, u32[]{:S(2)}, u32[]{:S(2)}) collective-permute-start(bf16[3,1,1,1,512]{4,2,1,0,3:T(2,128)(2,1)S(1)} %pad_maximum_fusion.5), channel_id=1, source_target_pairs={{2,0},{4,2},{6,4},{3,1},{5,3},{7,5},{10,8},{12,10},{14,12},{11,9},... | collective-permute-start | bytes 9224 | tf_op jit(solution)/shard_map/ppermute | solution.py:22
  108.6 9.9 %collective-permute-start.10 = (bf16[3,3,1,1,512]{4,2,1,0,3:T(2,128)(2,1)S(1)}, bf16[3,3,1,1,512]{4,2,1,0,3:T(2,128)(2,1)S(1)}, u32[]{:S(2)}, u32[]{:S(2)}) collective-permute-start(bf16[3,3,1,1,512]{4,2,1,0,3:T(2,128)(2,1)S(1)} %pad_maximum_fusion.4), channel_id=1, source_target_pairs={{0,1},{2,3},{4,5},{6,7},{8,9},{10,11},{12,13},{14,15},{16,17},{18,... | collective-permute-start | bytes 27656 | tf_op jit(solution)/shard_map/ppermute | solution.py:20
  111.1 7.4 %collective-permute-start.11 = (bf16[3,3,1,1,512]{4,2,1,0,3:T(2,128)(2,1)S(1)}, bf16[3,3,1,1,512]{4,2,1,0,3:T(2,128)(2,1)S(1)}, u32[]{:S(2)}, u32[]{:S(2)}) collective-permute-start(bf16[3,3,1,1,512]{4,2,1,0,3:T(2,128)(2,1)S(1)} %pad_maximum_fusion.4), channel_id=1, source_target_pairs={{1,0},{3,2},{5,4},{7,6},{9,8},{11,10},{13,12},{15,14},{17,16},{19,... | collective-permute-start | bytes 27656 | tf_op jit(solution)/shard_map/ppermute | solution.py:22
  112.4 21.1 %collective-permute-start.2 = (bf16[3,1,1,8,512]{4,3,2,1,0:T(8,128)(2,1)S(1)}, bf16[3,1,1,8,512]{4,3,2,1,0:T(8,128)(2,1)S(1)}, u32[]{:S(2)}, u32[]{:S(2)}) collective-permute-start(bf16[3,1,1,8,512]{4,3,2,1,0:T(8,128)(2,1)S(1)} %pad_maximum_fusion.3), channel_id=1, source_target_pairs={{0,2},{2,4},{4,6},{1,3},{3,5},{5,7},{8,10},{10,12},{12,14},{9,11},... | collective-permute-start | bytes 73736 | tf_op jit(solution)/shard_map/ppermute | solution.py:20
  114.7 18.8 %collective-permute-start.3 = (bf16[3,1,1,8,512]{4,3,2,1,0:T(8,128)(2,1)S(1)}, bf16[3,1,1,8,512]{4,3,2,1,0:T(8,128)(2,1)S(1)}, u32[]{:S(2)}, u32[]{:S(2)}) collective-permute-start(bf16[3,1,1,8,512]{4,3,2,1,0:T(8,128)(2,1)S(1)} %pad_maximum_fusion.3), channel_id=1, source_target_pairs={{2,0},{4,2},{6,4},{3,1},{5,3},{7,5},{10,8},{12,10},{14,12},{11,9},... | collective-permute-start | bytes 73736 | tf_op jit(solution)/shard_map/ppermute | solution.py:22
  132.8 12.9 %copy-start.8 = (f32[512]{0:T(512)}, f32[512]{0:T(512)S(1)}, u32[]{:S(2)}) copy-start(f32[512]{0:T(512)S(1)} %add.348) | copy-start | bytes 6148
  133.6 8.0 %collective-permute-start.4 = (bf16[3,3,1,8,512]{4,3,2,1,0:T(8,128)(2,1)S(1)}, bf16[3,3,1,8,512]{4,3,2,1,0:T(8,128)(2,1)S(1)}, u32[]{:S(2)}, u32[]{:S(2)}) collective-permute-start(bf16[3,3,1,8,512]{4,3,2,1,0:T(8,128)(2,1)S(1)} %pad_maximum_fusion.1), channel_id=1, source_target_pairs={{0,1},{2,3},{4,5},{6,7},{8,9},{10,11},{12,13},{14,15},{16,17},{18,... | collective-permute-start | bytes 221192 | tf_op jit(solution)/shard_map/ppermute | solution.py:20
  138.1 6.2 %collective-permute-start.5 = (bf16[3,3,1,8,512]{4,3,2,1,0:T(8,128)(2,1)S(1)}, bf16[3,3,1,8,512]{4,3,2,1,0:T(8,128)(2,1)S(1)}, u32[]{:S(2)}, u32[]{:S(2)}) collective-permute-start(bf16[3,3,1,8,512]{4,3,2,1,0:T(8,128)(2,1)S(1)} %pad_maximum_fusion.1), channel_id=1, source_target_pairs={{1,0},{3,2},{5,4},{7,6},{9,8},{11,10},{13,12},{15,14},{17,16},{19,... | collective-permute-start | bytes 221192 | tf_op jit(solution)/shard_map/ppermute | solution.py:22
  171.3 6.8 %copy-start = (bf16[64,2048]{1,0:T(8,128)(2,1)S(1)}, bf16[64,2048]{1,0:T(8,128)(2,1)}, u32[]{:S(2)}) copy-start(bf16[64,2048]{1,0:T(8,128)(2,1)} %reshape.826) | copy-start | bytes 786436
  171.8 5.9 %copy-start.2 = (bf16[64,2048]{1,0:T(8,128)(2,1)S(1)}, bf16[64,2048]{1,0:T(8,128)(2,1)}, u32[]{:S(2)}) copy-start(bf16[64,2048]{1,0:T(8,128)(2,1)} %reshape.824) | copy-start | bytes 786436
  171.8 6.2 %copy-start.1 = (bf16[64,2048]{1,0:T(8,128)(2,1)S(1)}, bf16[64,2048]{1,0:T(8,128)(2,1)}, u32[]{:S(2)}) copy-start(bf16[64,2048]{1,0:T(8,128)(2,1)} %reshape.825) | copy-start | bytes 786436
where the time goes:
time: 181 us; the launch traced here: 180 us
  matrix products  64.1 us (35%)
  blocking collectives  41.2 us (23%)
  starting transfers between devices  32.6 us (18%)
  local copies, waits for them, and re-layouts  28 us (15%)
  other arithmetic  5.35 us (3%)
  waiting for transfers between devices  5.27 us (3%)
  between operations  3.01 us (2%)
    psum x1, blocking collectives, shards(): coarse_source = lax.psum(partial_sum, ('gx', 'gy', 'gz'))  41.2 us
    reshape x27, local copies, waits for them, and re-layouts, apply_boxes(): flat_terms = mixed_terms.reshape(box_count * basis_order, -1)  19.5 us
    dot_general x27, matrix products, apply_boxes(): jnp.dot(flat_terms, blocks[along_y, along_z], preferred_element_type=jnp....  18.6 us
    ppermute x6, starting transfers between devices, padded_2(): lax.ppermute(tail, axis, [(i, (i + 1) % count) for i in range(ends)])  16.5 us
    ppermute x6, starting transfers between devices, padded_2(): lax.ppermute(head, axis, [((i + 1) % count, i) for i in range(ends)])  16.1 us
    dot_general x27, matrix products, apply_boxes(): jnp.einsum('mdax,bdxq->bamq', factor_bf, picked, preferred_element_type=j...  12.5 us
    dot_general x4, matrix products, prolong(): jnp.einsum('bijxyr,lrz->bijlxyz', section_two, filters, precision=exact_m...  8.2 us
    unnamed x6, matrix products  7.83 us
  transfers between devices with their start and end apart: 12, of which 2 were waited for; matrix products, arithmetic and copies ran while one was open for 27% of the time, Pallas kernels for 0%

commit v1 on v0

v1 whole, which is shorter than its diff:
```python
import math

import jax
import jax.numpy as jnp
import numpy as np
from jax import lax
from jax.experimental import pallas as pl
from jax.experimental.pallas import tpu as pltpu
from jax.sharding import PartitionSpec as P

exact_mode = lax.Precision.HIGHEST


def poly_multiply(left, right):
    result = [0.0] * (len(left) + len(right) - 1)
    for first, left_coef in enumerate(left):
        for second, right_coef in enumerate(right):
            result[first + second] += left_coef * right_coef
    return result


def poly_compose(coeffs, factor, offset):
    result = [0.0]
    power_term = [1.0]
    for coef in coeffs:
        padded = result + [0.0] * (len(power_term) - len(result))
        result = [padded[place] + coef * power_term[place] for place in range(len(power_term))]
        power_term = poly_multiply(power_term, [offset, factor])
    return result


def legendre_table(basis_order):
    polys = [[1.0], [0.0, 1.0]]
    for degree in range(1, basis_order):
        upper = [0.0] + [(2 * degree + 1) * coef for coef in polys[degree]]
        lower = [degree * coef for coef in polys[degree - 1]] + [0.0] * (
            len(upper) - len(polys[degree - 1])
        )
        polys.append([(upper[place] - lower[place]) / (degree + 1) for place in range(len(upper))])
    return [
        [math.sqrt(2 * degree + 1) * coef for coef in poly_compose(polys[degree], 2.0, -1.0)]
        for degree in range(basis_order)
    ]


def two_scale(basis_order):
    shifted = legendre_table(basis_order)
    filters = np.zeros((2, basis_order, basis_order))
    for which_half in range(2):
        for row_at in range(basis_order):
            halved = poly_compose(shifted[row_at], 0.5, 0.5 * which_half)
            for col_at in range(basis_order):
                product = poly_multiply(halved, shifted[col_at])
                total = sum((coef / (place + 1) for place, coef in enumerate(product)))
                filters[which_half, row_at, col_at] = total / math.sqrt(2.0)
    return jnp.asarray(filters, jnp.float32)


def compress(children, filters):
    box_count = children.shape[0]
    basis_order = filters.shape[1]
    cube_form = children.reshape(box_count, 2, 2, 2, basis_order, basis_order, basis_order)
    section_one = jnp.einsum("bijlxyz,ipx->bjlpyz", cube_form, filters, precision=exact_mode)
    section_two = jnp.einsum("bjlpyz,jqy->blpqz", section_one, filters, precision=exact_mode)
    section_three = jnp.einsum("blpqz,lrz->bpqr", section_two, filters, precision=exact_mode)
    return section_three.reshape(box_count, basis_order**3)


def prolong(parents, filters):
    box_count = parents.shape[0]
    basis_order = filters.shape[1]
    cube_form = parents.reshape(box_count, basis_order, basis_order, basis_order)
    section_one = jnp.einsum("bpqr,ipx->bixqr", cube_form, filters, precision=exact_mode)
    section_two = jnp.einsum("bixqr,jqy->bijxyr", section_one, filters, precision=exact_mode)
    section_three = jnp.einsum("bijxyr,lrz->bijlxyz", section_two, filters, precision=exact_mode)
    return section_three.reshape(box_count, 8, basis_order**3)


def local_rows(near_ids, per_device):
    size_y = lax.axis_size("gy")
    size_z = lax.axis_size("gz")
    mine_x = lax.axis_index("gx")
    mine_y = lax.axis_index("gy")
    mine_z = lax.axis_index("gz")
    device = near_ids // per_device
    slot_at = near_ids % per_device
    other_x = device // (size_y * size_z)
    other_y = device // size_z % size_y
    other_z = device % size_z
    cell_at = (other_x - mine_x + 1) * 9 + (other_y - mine_y + 1) * 3 + (other_z - mine_z + 1)
    return jnp.where(near_ids >= 0, cell_at * per_device + slot_at, -1)


MESH = pl.DeviceIdType.MESH
AXES = ("gx", "gy", "gz")
CHUNK = 4


def exchange_kernel(sizes, fine_ref, row_ref, halo, rows, own_sem, fs, fr, ms, mr):
    here = [lax.axis_index(axis) for axis in AXES]

    def peer(dim, offset):
        spot = list(here)
        spot[dim] = lax.rem(here[dim] + offset, sizes[dim])
        return tuple(spot)

    barrier = pltpu.get_barrier_semaphore()
    for dim in range(3):
        for offset in range(1, sizes[dim]):
            pl.semaphore_signal(barrier, inc=1, device_id=peer(dim, offset), device_id_type=MESH)
    own = [
        pltpu.make_async_copy(fine_ref, halo.at[1, 1, 1], own_sem.at[0]),
        pltpu.make_async_copy(row_ref, rows.at[here[0], here[1], here[2]], own_sem.at[1]),
    ]
    for copy in own:
        copy.start()
    for copy in own:
        copy.wait()
    pl.semaphore_wait(barrier, sum(sizes) - 3)
    views = (
        lambda k: halo.at[k],
        lambda k: halo.at[1, k],
        lambda k: halo.at[1, 1, k],
    )
    mine = (
        rows.at[here[0]],
        rows.at[here[0], here[1]],
        rows.at[here[0], here[1], here[2]],
    )
    for dim in (2, 1, 0):
        copies = []
        for side, (offset, land) in enumerate(((1, 0), (sizes[dim] - 1, 2))):
            copies.append(
                pltpu.make_async_remote_copy(
                    src_ref=views[dim](1),
                    dst_ref=views[dim](land),
                    send_sem=fs.at[dim, side],
                    recv_sem=fr.at[dim, side],
                    device_id=peer(dim, offset),
                    device_id_type=MESH,
                )
            )
        for offset in range(1, sizes[dim]):
            copies.append(
                pltpu.make_async_remote_copy(
                    src_ref=mine[dim],
                    dst_ref=mine[dim],
                    send_sem=ms.at[dim, offset],
                    recv_sem=mr.at[dim, offset],
                    device_id=peer(dim, offset),
                    device_id_type=MESH,
                )
            )
        for copy in copies:
            copy.start()
        for copy in copies:
            copy.wait()


def exchange(fine_detail, row):
    sizes = tuple(lax.axis_size(axis) for axis in AXES)
    most = max(sizes)
    vmem = pl.BlockSpec(memory_space=pltpu.VMEM)
    dma = pltpu.SemaphoreType.DMA
    return pl.pallas_call(
        lambda *refs: exchange_kernel(sizes, *refs),
        out_shape=(
            jax.ShapeDtypeStruct((3, 3, 3) + fine_detail.shape, fine_detail.dtype),
            jax.ShapeDtypeStruct(sizes + row.shape, row.dtype),
        ),
        in_specs=[vmem, vmem],
        out_specs=(vmem, vmem),
        scratch_shapes=[dma((2,)), dma((3, 2)), dma((3, 2)), dma((3, most)), dma((3, most))],
        compiler_params=pltpu.CompilerParams(collective_id=0, has_side_effects=True),
        name="exchange",
    )(fine_detail, row)


def apply_kernel(left_ref, right_ref, mix_ref, *refs):
    levels = mix_ref.shape[0]
    chunks, terms = left_ref.shape[1], mix_ref.shape[2]
    lanes = CHUNK * 64
    sources, outs, sums = refs[:levels], refs[levels : 2 * levels], refs[2 * levels :]
    pair = lax.broadcasted_iota(jnp.int32, (CHUNK * 8, lanes), 0)
    lane = lax.broadcasted_iota(jnp.int32, (CHUNK * 8, lanes), 1)
    same_term = pair // 8 == lane // 64
    outer = (same_term & (pair % 8 == lane // 8 % 8)).astype(jnp.float32)
    inner = (same_term & (pair % 8 == lane % 8)).astype(jnp.float32)
    term = lax.broadcasted_iota(jnp.int32, (terms, lanes), 0)
    term_lane = lax.broadcasted_iota(jnp.int32, (terms, lanes), 1) // 64
    for level in range(levels):
        total = sums[level]
        boxes = total.shape[1]
        total[...] = jnp.zeros_like(total)

        def step(c, carry, level=level, total=total, boxes=boxes):
            left = jnp.dot(left_ref[level, c], outer, precision=exact_mode,
                           preferred_element_type=jnp.float32)
            right = jnp.dot(right_ref[level, c], inner, precision=exact_mode,
                            preferred_element_type=jnp.float32)
            pick = (term == term_lane + c * CHUNK).astype(jnp.float32).astype(jnp.bfloat16)
            mix = jnp.dot(mix_ref[level], pick, preferred_element_type=jnp.float32)
            blocks = []
            for ey in range(3):
                for ez in range(3):
                    block = (left[ey * 8 : ey * 8 + 8][:, None, :]
                             * right[ez * 8 : ez * 8 + 8][None, :, :])
                    blocks.append(block.reshape(64, lanes).astype(jnp.bfloat16))
            table = jnp.concatenate(blocks, axis=0)
            spread = jnp.dot(sources[level][...], table, preferred_element_type=jnp.float32)
            spread = spread.reshape(boxes, 3, 8, lanes)
            for a in range(8):
                factor = mix[a * 24 : a * 24 + 24].reshape(3, 8, lanes)
                total[a] += jnp.sum(spread * factor[None], axis=1)
            return carry

        lax.fori_loop(0, chunks, step, 0)
        for a in range(8):
            folded = jnp.sum(total[a], axis=1)
            result = folded[:, :64]
            for k in range(1, CHUNK):
                result = result + folded[:, k * 64 : k * 64 + 64]
            outs[level][a] = result


def apply_levels(factors, weights, sources):
    levels, terms = factors.shape[:2]
    chunks = terms // CHUNK
    right = jnp.transpose(
        factors.reshape(levels, chunks, CHUNK, 3, 8, 8), (0, 1, 3, 5, 2, 4)
    )
    left = right * weights.reshape(1, chunks, 1, 1, CHUNK, 1)
    right = right.reshape(levels, chunks, 24, CHUNK * 8)
    left = left.reshape(levels, chunks, 24, CHUNK * 8)
    mix = jnp.transpose(factors.astype(jnp.bfloat16), (0, 3, 2, 4, 1)).reshape(
        levels, 192, terms
    )
    counts = [source.shape[0] // 24 for source in sources]
    vmem = pl.BlockSpec(memory_space=pltpu.VMEM)
    outs = pl.pallas_call(
        apply_kernel,
        out_shape=tuple(jax.ShapeDtypeStruct((8, n, 64), jnp.float32) for n in counts),
        in_specs=[vmem] * (3 + levels),
        out_specs=tuple(vmem for _ in counts),
        scratch_shapes=[pltpu.VMEM((8, n, 8, CHUNK * 64), jnp.float32) for n in counts],
        name="apply_levels",
    )(left, right, mix, *sources)
    return [
        jnp.transpose(out, (1, 0, 2)).reshape(n, 512) for out, n in zip(outs, counts)
    ]


def pick_sources(table, ids):
    boxes = ids.shape[0]
    picked = table[jnp.maximum(ids, 0)] * (ids >= 0)[:, :, None].astype(jnp.bfloat16)
    picked = picked.reshape(boxes, 3, 9, 8, 64)
    return jnp.transpose(picked, (0, 1, 3, 2, 4)).reshape(boxes * 24, 576)


def shards(
    fine_coef,
    mid_leaf,
    mid_child,
    mid_parent,
    mid_refined,
    fine_nbr,
    mid_nbr,
    coarse_nbr,
    op_factor,
    term_weight,
):
    basis_order = op_factor.shape[-1]
    filters = two_scale(basis_order)
    mid_local = mid_child.shape[0]
    slots_dev = fine_coef.shape[0]
    coarse_count = coarse_nbr.shape[0]
    child_hot = (
        mid_child[:, :, None] == jnp.arange(slots_dev, dtype=jnp.int32)[None, None, :]
    ).astype(jnp.float32)
    refined = mid_refined.astype(jnp.float32)
    live_mask = jnp.sum(child_hot * refined[:, None, None], axis=(0, 1))
    children = fine_coef[mid_child].astype(jnp.float32)
    compressed = compress(children, filters)
    mid_source = jnp.where(
        mid_refined[:, None] > 0, compressed, mid_leaf.astype(jnp.float32)
    ).astype(jnp.bfloat16)
    mid_float = mid_source.astype(jnp.float32)
    spread = prolong(mid_float, filters)
    fine_from = jnp.einsum("mos,mok->sk", child_hot, spread, precision=exact_mode)
    fine_detail = (live_mask[:, None] * (fine_coef.astype(jnp.float32) - fine_from)).astype(
        jnp.bfloat16
    )
    parent = mid_parent // 8
    octant = mid_parent % 8
    place = jnp.stack([parent, octant], axis=1).astype(jnp.bfloat16)
    row = jnp.concatenate(
        [mid_source, jnp.pad(place, ((0, 0), (0, 510)))], axis=1
    ).reshape(mid_local, 8, 128)
    halo, rows = exchange(fine_detail, row)
    rows = rows.reshape(-1, 1024)
    mid_all = rows[:, :512]
    place_all = rows[:, 512:514].astype(jnp.int32)
    parent_all = place_all[:, 0] * 8 + place_all[:, 1]
    slot_hot = (
        jnp.arange(coarse_count * 8, dtype=jnp.int32)[:, None] == parent_all[None, :]
    ).astype(jnp.bfloat16)
    slots = jnp.dot(slot_hot, mid_all, preferred_element_type=jnp.float32)
    coarse_source = compress(slots.reshape(coarse_count, 8, 512), filters)
    from_coarse = prolong(coarse_source, filters).reshape(coarse_count * 8, 512)
    mid_table = (slots - from_coarse).astype(jnp.bfloat16)
    coarse_table = coarse_source.astype(jnp.bfloat16)
    fine_picked = pick_sources(halo.reshape(-1, 512), local_rows(fine_nbr, slots_dev))
    near_slot = jnp.where(mid_nbr >= 0, parent_all[jnp.maximum(mid_nbr, 0)], -1)
    mid_picked = pick_sources(mid_table, near_slot)
    coarse_picked = pick_sources(coarse_table, coarse_nbr[parent])
    fine_direct, mid_direct, parent_out = apply_levels(
        op_factor, term_weight, [fine_picked, mid_picked, coarse_picked]
    )
    octant_hot = (octant[:, None] == jnp.arange(8, dtype=jnp.int32)[None, :]).astype(jnp.float32)
    mid_out = mid_direct + jnp.sum(
        octant_hot[:, :, None] * prolong(parent_out, filters), axis=1
    )
    fine_back = jnp.einsum(
        "mos,mok->sk", child_hot, prolong(mid_out, filters), precision=exact_mode
    )
    fine_out = live_mask[:, None] * (fine_direct + fine_back)
    return (fine_out, mid_out)


def solution(mesh):
    return jax.shard_map(
        shards,
        mesh=mesh,
        in_specs=(
            P(("gx", "gy", "gz"), None),
            P(("gx", "gy", "gz"), None),
            P(("gx", "gy", "gz"), None),
            P(("gx", "gy", "gz")),
            P(("gx", "gy", "gz")),
            P(("gx", "gy", "gz"), None),
            P(("gx", "gy", "gz"), None),
            P(),
            P(),
            P(),
        ),
        out_specs=(P(("gx", "gy", "gz"), None), P(("gx", "gy", "gz"), None)),
        check_vma=False,
    )
```

time: 181 us -> 70.8 us (0.39)
  the two profiles are of different devices: /device:TPU:10 before, /device:TPU:0 now
where the time goes in v1:
time: 70.8 us; the launch traced here: 70.4 us
  Pallas kernels  29.3 us (41%)
  local copies, waits for them, and re-layouts  19 us (27%)
  matrix products  14.8 us (21%)
  other arithmetic  4.77 us (7%)
  between operations  2.58 us (4%)
    pallas_call x1, Pallas kernels, exchange(): pl.pallas_call(lambda *refs: exchange_kernel(sizes, *refs), out_shape=(ja...  16.8 us
    pallas_call x1, Pallas kernels, apply_levels(): pl.pallas_call(apply_kernel, out_shape=tuple((jax.ShapeDtypeStruct((8, n,...  12.5 us
    dot_general x4, matrix products, prolong(): jnp.einsum('bijxyr,lrz->bijlxyz', section_two, filters, precision=exact_m...  6.65 us
    gather x6, local copies, waits for them, and re-layouts, pick_sources(): table[jnp.maximum(ids, 0)] * (ids >= 0)[:, :, None].astype(jnp.bfloat16)  3.75 us
    pallas_call x2, other arithmetic, apply_levels(): pl.pallas_call(apply_kernel, out_shape=tuple((jax.ShapeDtypeStruct((8, n,...  2.69 us
    reshape x3, local copies, waits for them, and re-layouts, pick_sources(): return jnp.transpose(picked, (0, 1, 3, 2, 4)).reshape(boxes * 24, 576)  2.56 us
    dot_general x2, matrix products, compress(): jnp.einsum('bijlxyz,ipx->bjlpyz', cube_form, filters, precision=exact_mode)  2.07 us
    unnamed x39, local copies, waits for them, and re-layouts  1.6 us

profile of v1, /device:TPU:0, one launch (start us, length us, event | category | flops | bytes accessed | tf_op | source)
XLA Modules:
  0.0 70.4 jit_solution(12465901731136205472)
XLA Ops:
  0.6 1.4 %copy.96 = f32[3,32,3,8,8]{4,3,2,1,0:T(8,128)S(1)} copy(f32[3,32,3,8,8]{1,4,3,2,0:T(8,128)} %param.19) | data formatting | bytes 147456 | tf_op args[8]
  2.3 0.6 copy.97
  2.9 1.2 %reshape.443.left_ref = f32[3,8,24,32]{3,2,1,0:T(8,128)} reshape(f32[3,8,3,8,4,8]{5,4,3,2,1,0:T(4,128)S(1)} %copy.97) | data formatting | bytes 147456 | tf_op jit(solution)/shard_map/reshape | solution.py:234
  4.2 0.6 copy.98
  4.9 1.2 %reshape.444.right_ref = f32[3,8,24,32]{3,2,1,0:T(8,128)} reshape(f32[3,8,3,8,4,8]{5,4,3,2,1,0:T(4,128)S(1)} %copy.98) | data formatting | bytes 147456 | tf_op jit(solution)/shard_map/reshape | solution.py:233
  6.1 0.7 copy.99
  6.8 0.6 gather_fusion
  7.4 0.2 reshape.446
  7.6 0.3 convolution_bitcast_fusion.8
  7.9 0.3 convolution_bitcast_fusion.12
  8.2 0.2 convolution_bitcast_fusion.13
  9.3 0.2 fusion.30
  9.5 0.3 convolution_bitcast_fusion.11
  9.8 1.9 %convolution_bitcast_fusion.7 = f32[1,2,2,2,8,8,8]{5,6,4,2,1,3,0:T(8,128)S(1)} fusion(f32[2,8,8,1,1,1]{2,1,5,4,3,0:T(8,128)S(1)} %copy-done.4, f32[2,2,8,8,8]{4,3,2,0,1:T(8,128)S(1)} %convolution_bitcast_fusion.11), kind=kOutput, calls=%fused_computation.12 | convolution fusion | flops 393216 | bytes 25088 | tf_op jit(solution)/shard_map/bijxyr,lrz->bijlxyz/dot_general | solution.py:75
  12.1 0.9 %fusion.2.refs_0_ = bf16[8,512]{1,0:T(8,128)(2,1)} fusion(f32[8,512]{1,0:T(8,128)S(1)} %reshape.452, bf16[8,512]{1,0:T(8,128)(2,1)S(1)} %copy-done.1, f32[8]{0:T(128)S(1)} %select_reduce_fusion, s32[8]{0:T(128)S(1)} %bitcast.230), kind=kOutput, calls=%fused_computation.23 | convolution fusion | flops 409664 | bytes 32832 | tf_op jit(solution)/shard_map/mos,mok->sk/dot_general | solution.py:289
  13.7 0.6 maximum_reduce_fusion
  14.3 16.8 %exchange.1 = (bf16[3,3,3,8,512]{4,3,2,1,0:T(8,128)(2,1)}, bf16[4,4,2,1,8,128]{5,4,3,2,1,0:T(8,128)(2,1)}) custom-call(bf16[8,512]{1,0:T(8,128)(2,1)} %fusion.2.refs_0_, bf16[1,8,128]{2,1,0:T(8,128)(2,1)} %bitcast.228), custom_call_target="tpu_custom_call" | custom-call | tf_op jit(solution)/shard_map/exchange/pallas_call | solution.py:165
  31.3 2.1 %gather_fusion.1 = bf16[216,512]{1,0:T(8,128)(2,1)S(1)} fusion(bf16[216,512]{1,0:T(8,128)(2,1)} %bitcast.217, s32[1024]{0:T(1024)S(1)} %pad_clamp_fusion.3), kind=kCustom, calls=%fused_computation.1 | custom fusion | bytes 443232 | tf_op jit(solution)/shard_map/gather | solution.py:255
  33.4 0.2 gather.26
  33.9 1.1 %reshape.455.refs_0_ = bf16[192,576]{1,0:T(8,128)(2,1)} reshape(bf16[8,3,8,9,64]{4,3,2,1,0:T(8,128)(2,1)S(1)} %fusion.4) | data formatting | bytes 442368 | tf_op jit(solution)/shard_map/reshape | solution.py:257
  35.2 0.6 reshape_reshape.6
  35.8 1.8 %convolution_bitcast_fusion.2 = f32[4,2,2,8,8,8]{3,5,4,2,1,0:T(8,128)S(1)} fusion(f32[2,8,8,1,1,1,1]{2,1,0,6,5,4,3:T(8,128)S(1)} %copy-done.7, f32[4,2,2,2,8,8,8]{6,5,4,3,2,1,0:T(8,128)S(1)} %reshape_reshape.6), kind=kOutput, calls=%fused_computation.7 | convolution fusion | flops 1572864 | bytes 98816 | tf_op jit(solution)/shard_map/bijlxyz,ipx->bjlpyz/dot_general | solution.py:63
  37.7 0.5 copy.112
  38.2 0.5 convolution_bitcast_fusion.3
  38.8 0.6 bitcast_convert_fusion
  39.4 0.4 convolution_bitcast_fusion.6
  39.8 0.2 copy.150
  40.0 0.6 convolution_bitcast_fusion.1
  40.5 1.0 %convolution_bitcast_fusion = f32[4,2,2,2,8,8,8]{6,5,3,4,2,1,0:T(8,128)S(1)} fusion(f32[4,2,2,8,8,8,1]{4,5,6,3,2,1,0:T(8,128)S(1)} %convolution_bitcast_fusion.1, f32[2,8,8,1,1,1,1]{2,1,0,6,5,4,3:T(8,128)S(1)} %copy-done.7), kind=kOutput, calls=%fused_computation.5 | convolution fusion | flops 1572864 | bytes 98816 | tf_op jit(solution)/shard_map/bijxyr,lrz->bijlxyz/dot_general | solution.py:75
  41.7 0.5 reshape_reshape.7
  42.3 0.7 gather_fusion.2
  43.0 0.6 gather_fusion.3
  44.0 0.7 %reshape.457.refs_1_ = bf16[24,576]{1,0:T(8,128)(2,1)} reshape(bf16[1,3,8,9,64]{4,3,2,1,0:T(8,128)(2,1)S(1)} %fusion.15) | data formatting | bytes 55296 | tf_op jit(solution)/shard_map/reshape | solution.py:257
  44.8 0.6 gather_fusion.4
  45.7 0.7 %reshape.458.refs_2_ = bf16[24,576]{1,0:T(8,128)(2,1)} reshape(bf16[1,3,8,9,64]{4,3,2,1,0:T(8,128)(2,1)S(1)} %fusion.14) | data formatting | bytes 55296 | tf_op jit(solution)/shard_map/reshape | solution.py:257
  46.5 12.5 %apply_levels.1 = (f32[8,8,64]{2,1,0:T(8,128)}, f32[8,1,64]{2,1,0:T(1,128)}, f32[8,1,64]{2,1,0:T(1,128)}) custom-call(f32[3,8,24,32]{3,2,1,0:T(8,128)} %reshape.443.left_ref, f32[3,8,24,32]{3,2,1,0:T(8,128)} %reshape.444.right_ref, bf16[3,192,32]{2,1,0:T(8,128)(2,1)} %bitcast.220, bf16[192,576]{1,0:T(8,128)(2,1)} %reshape.455.refs_0_, ...), custom_call_target="tpu_custom_call" | custom-call | tf_op jit(solution)/shard_map/apply_levels/pallas_call | solution.py:240
  59.0 0.8 %copy.120 = f32[8,8,64]{2,1,0:T(8,128)S(1)} copy(f32[8,8,64]{2,0,1:T(8,128)} %bitcast.225) | data formatting | bytes 32768 | tf_op jit(solution)/shard_map/transpose | solution.py:249
  59.8 0.5 broadcast.280
  60.3 1.3 %reduce.20 = f32[8,64]{1,0:T(8,128)S(1)} reduce(f32[8,1,64]{2,1,0:T(1,128)} %get-tuple-element.10, f32[]{:T(128)} %broadcast.280), dimensions={1}, to_apply=%get-tuple-element.10.reduce_sub_computation.5 | reduce | bytes 4100 | tf_op jit(solution)/shard_map/apply_levels/pallas_call | solution.py:240
  61.7 1.4 %reduce.21 = f32[8,64]{1,0:T(8,128)S(1)} reduce(f32[8,1,64]{2,1,0:T(1,128)} %get-tuple-element.11, f32[]{:T(128)} %broadcast.280), dimensions={1}, to_apply=%get-tuple-element.11.reduce_sub_computation.3 | reduce | bytes 4100 | tf_op jit(solution)/shard_map/apply_levels/pallas_call | solution.py:240
  63.2 0.3 fusion.26
  63.4 0.3 convolution_bitcast_fusion.10
  63.7 1.9 %convolution_bitcast_fusion.5 = f32[1,2,2,2,8,8,8]{5,6,4,2,1,3,0:T(8,128)S(1)} fusion(f32[2,8,8,1,1,1]{2,1,5,4,3,0:T(8,128)S(1)} %copy-done.4, f32[2,2,8,8,8]{4,3,2,0,1:T(8,128)S(1)} %convolution_bitcast_fusion.10), kind=kOutput, calls=%fused_computation.10 | convolution fusion | flops 393216 | bytes 25088 | tf_op jit(solution)/shard_map/bijxyr,lrz->bijlxyz/dot_general | solution.py:75
  66.1 0.3 fusion.24
  66.4 0.3 convolution_bitcast_fusion.9
  66.7 1.9 %convolution_bitcast_fusion.4 = f32[1,2,2,2,8,8,8]{5,6,4,2,1,3,0:T(8,128)S(1)} fusion(f32[2,8,8,1,1,1]{2,1,5,4,3,0:T(8,128)S(1)} %copy-done.4, f32[2,2,8,8,8]{4,3,2,0,1:T(8,128)S(1)} %convolution_bitcast_fusion.9), kind=kOutput, calls=%fused_computation.9 | convolution fusion | flops 393216 | bytes 25088 | tf_op jit(solution)/shard_map/bijxyr,lrz->bijlxyz/dot_general | solution.py:75
  68.9 0.9 %fusion = f32[8,512]{1,0:T(8,128)} fusion(f32[8,512]{1,0:T(8,128)S(1)} %reshape.459, f32[8,512]{1,0:T(8,128)S(1)} %reshape.464, f32[8]{0:T(128)S(1)} %select_reduce_fusion, s32[8]{0:T(128)S(1)} %bitcast.231), kind=kOutput, calls=%fused_computation.20 | convolution fusion | flops 401472 | bytes 49216 | tf_op jit(solution)/shard_map/mos,mok->sk/dot_general | solution.py:323
  69.8 0.6 add.99
  (88 shorter events, 3.5 us)
Async XLA Ops:
  0.6 1.4 %copy-start.14 = (f32[32]{0:T(128)S(1)}, f32[32]{0:T(128)}, u32[]{:S(2)}) copy-start(f32[32]{0:T(128)} %param.20) | copy-start | bytes 388
  4.8 1.3 %copy-start = (f32[3,32,3,8,8]{1,4,3,2,0:T(8,128)S(1)}, f32[3,32,3,8,8]{1,4,3,2,0:T(8,128)}, u32[]{:S(2)}) copy-start(f32[3,32,3,8,8]{1,4,3,2,0:T(8,128)} %param.19) | copy-start | bytes 221188
  4.8 2.0 %copy-start.17 = (s32[1,8]{1,0:T(1,128)S(1)}, s32[1,8]{1,0:T(1,128)}, u32[]{:S(2)}) copy-start(s32[1,8]{1,0:T(1,128)} %param.13) | copy-start | bytes 100
  4.8 2.0 %copy-start.1 = (bf16[8,512]{1,0:T(8,128)(2,1)S(1)}, bf16[8,512]{1,0:T(8,128)(2,1)}, u32[]{:S(2)}) copy-start(bf16[8,512]{1,0:T(8,128)(2,1)} %param.11) | copy-start | bytes 24580
  4.8 2.8 %copy-start.11 = (f32[2,8,8,1,1,1]{2,1,0,5,4,3:T(8,128)S(1)}, f32[2,8,8,1,1,1]{2,1,0,5,4,3:T(8,128)}, u32[]{:S(2)}) copy-start(f32[2,8,8,1,1,1]{2,1,0,5,4,3:T(8,128)} %constant.167) | copy-start | bytes 1540
  4.8 3.1 %copy-start.3 = (f32[2,8,8,1,1]{2,1,0,4,3:T(8,128)S(1)}, f32[2,8,8,1,1]{2,1,0,4,3:T(8,128)}, u32[]{:S(2)}) copy-start(f32[2,8,8,1,1]{2,1,0,4,3:T(8,128)} %constant.166) | copy-start | bytes 1540
  4.8 3.3 %copy-start.2 = (f32[2,8,8,1]{2,1,3,0:T(8,128)S(1)}, f32[2,8,8,1]{2,1,3,0:T(8,128)}, u32[]{:S(2)}) copy-start(f32[2,8,8,1]{2,1,3,0:T(8,128)} %constant.165) | copy-start | bytes 1540
  4.9 4.3 %copy-start.13 = (bf16[1,512]{1,0:T(2,128)(2,1)S(1)}, bf16[1,512]{1,0:T(2,128)(2,1)}, u32[]{:S(2)}) copy-start(bf16[1,512]{1,0:T(2,128)(2,1)} %param.12) | copy-start | bytes 3076
  6.1 3.4 %copy-start.5 = (f32[2,8,8,1,1]{2,1,4,3,0:T(8,128)S(1)}, f32[2,8,8,1,1]{2,1,4,3,0:T(8,128)}, u32[]{:S(2)}) copy-start(f32[2,8,8,1,1]{2,1,4,3,0:T(8,128)} %constant.164) | copy-start | bytes 1540
  6.1 3.7 %copy-start.4 = (f32[2,8,8,1,1,1]{2,1,5,4,3,0:T(8,128)S(1)}, f32[2,8,8,1,1,1]{2,1,5,4,3,0:T(8,128)}, u32[]{:S(2)}) copy-start(f32[2,8,8,1,1,1]{2,1,5,4,3,0:T(8,128)} %constant.163) | copy-start | bytes 1540
  7.6 23.5 %copy-start.12 = (s32[8,27]{1,0:T(8,128)S(1)}, s32[8,27]{1,0:T(8,128)}, u32[]{:S(2)}) copy-start(s32[8,27]{1,0:T(8,128)} %param.16) | copy-start | bytes 2596
  33.6 1.3 %copy-start.6 = (bf16[4,4,2,1,8,128]{5,4,3,2,1,0:T(8,128)(2,1)S(1)}, bf16[4,4,2,1,8,128]{5,4,3,2,1,0:T(8,128)(2,1)}, u32[]{:S(2)}) copy-start(bf16[4,4,2,1,8,128]{5,4,3,2,1,0:T(8,128)(2,1)} %get-tuple-element.8) | copy-start | bytes 196612
  33.9 2.0 %copy-start.7 = (f32[2,8,8,1,1,1,1]{2,1,0,6,5,4,3:T(8,128)S(1)}, f32[2,8,8,1,1,1,1]{2,1,0,6,5,4,3:T(8,128)}, u32[]{:S(2)}) copy-start(f32[2,8,8,1,1,1,1]{2,1,0,6,5,4,3:T(8,128)} %constant.168) | copy-start | bytes 1540
  35.8 2.4 %copy-start.10 = (f32[2,8,8,1,1,1]{2,1,0,4,5,3:T(8,128)S(1)}, f32[2,8,8,1,1,1]{2,1,0,4,5,3:T(8,128)}, u32[]{:S(2)}) copy-start(f32[2,8,8,1,1,1]{2,1,0,4,5,3:T(8,128)} %constant.169) | copy-start | bytes 1540
  38.2 1.8 %copy-start.9 = (f32[2,8,8,1,1,1]{2,1,5,0,4,3:T(8,128)S(1)}, f32[2,8,8,1,1,1]{2,1,5,0,4,3:T(8,128)}, u32[]{:S(2)}) copy-start(f32[2,8,8,1,1,1]{2,1,5,0,4,3:T(8,128)} %constant.170) | copy-start | bytes 1540
  41.6 0.7 copy-start.15
  41.7 2.0 %copy-start.16 = (s32[4,27]{1,0:T(4,128)S(1)}, s32[4,27]{1,0:T(4,128)}, u32[]{:S(2)}) copy-start(s32[4,27]{1,0:T(4,128)} %param.18) | copy-start | bytes 1300
  65.6 4.1 %copy-start.8 = (f32[8,1,64]{2,1,0:T(1,128)S(1)}, f32[8,1,64]{2,1,0:T(1,128)}, u32[]{:S(2)}) copy-start(f32[8,1,64]{2,1,0:T(1,128)} %get-tuple-element.10) | copy-start | bytes 6148

commit v2 on v1

--- a/solution.py
+++ b/solution.py
@@ -53,7 +53,7 @@
                 product = poly_multiply(halved, shifted[col_at])
                 total = sum((coef / (place + 1) for place, coef in enumerate(product)))
                 filters[which_half, row_at, col_at] = total / math.sqrt(2.0)
-    return jnp.asarray(filters, jnp.float32)
+    return np.asarray(filters, np.float32)
 
 
 def compress(children, filters):
@@ -176,11 +176,12 @@
     )(fine_detail, row)
 
 
-def apply_kernel(left_ref, right_ref, mix_ref, *refs):
+def apply_kernel(right_ref, weight_ref, mix_ref, wide_ref, tall_ref, live_ref, child_ref, octant_ref, *refs):
     levels = mix_ref.shape[0]
-    chunks, terms = left_ref.shape[1], mix_ref.shape[2]
+    chunks, terms = right_ref.shape[1], mix_ref.shape[2]
     lanes = CHUNK * 64
-    sources, outs, sums = refs[:levels], refs[levels : 2 * levels], refs[2 * levels :]
+    sources, (fine_ref, mid_ref), sums = refs[:levels], refs[levels : levels + 2], refs[levels + 2 :]
+    applied = []
     pair = lax.broadcasted_iota(jnp.int32, (CHUNK * 8, lanes), 0)
     lane = lax.broadcasted_iota(jnp.int32, (CHUNK * 8, lanes), 1)
     same_term = pair // 8 == lane // 64
@@ -194,7 +195,7 @@
         total[...] = jnp.zeros_like(total)
 
         def step(c, carry, level=level, total=total, boxes=boxes):
-            left = jnp.dot(left_ref[level, c], outer, precision=exact_mode,
+            left = jnp.dot(right_ref[level, c] * weight_ref[c], outer, precision=exact_mode,
                            preferred_element_type=jnp.float32)
             right = jnp.dot(right_ref[level, c], inner, precision=exact_mode,
                             preferred_element_type=jnp.float32)
@@ -215,39 +216,73 @@
             return carry
 
         lax.fori_loop(0, chunks, step, 0)
+        planes = []
         for a in range(8):
             folded = jnp.sum(total[a], axis=1)
             result = folded[:, :64]
             for k in range(1, CHUNK):
                 result = result + folded[:, k * 64 : k * 64 + 64]
-            outs[level][a] = result
-
-
-def apply_levels(factors, weights, sources):
+            planes.append(result)
+        applied.append(jnp.stack(planes, axis=1))
+
+    def children(block):
+        wide = jnp.dot(block, wide_ref[...], precision=exact_mode,
+                       preferred_element_type=jnp.float32)
+        tall = jnp.dot(tall_ref[...], wide, precision=exact_mode,
+                       preferred_element_type=jnp.float32)
+        return [
+            tall[o // 4 * 8 : o // 4 * 8 + 8, o % 4 * 64 : o % 4 * 64 + 64] for o in range(8)
+        ]
+
+    fine_direct, mid_direct, parent_out = applied
+    slots, mids = fine_direct.shape[0], mid_direct.shape[0]
+    totals = [fine_direct[slot] for slot in range(slots)]
+    for m in range(mids):
+        mid_out = mid_direct[m]
+        for o, block in enumerate(children(parent_out[m])):
+            mid_out = mid_out + octant_ref[m, o] * block
+        mid_ref[m] = mid_out
+        for o, block in enumerate(children(mid_out)):
+            for slot in range(slots):
+                totals[slot] = totals[slot] + child_ref[m * 8 + o, slot] * block
+    for slot in range(slots):
+        fine_ref[slot] = live_ref[0, slot] * totals[slot]
+
+
+def apply_levels(factors, weights, sources, live_mask, child_hot, octant_hot, filters):
     levels, terms = factors.shape[:2]
     chunks = terms // CHUNK
     right = jnp.transpose(
         factors.reshape(levels, chunks, CHUNK, 3, 8, 8), (0, 1, 3, 5, 2, 4)
-    )
-    left = right * weights.reshape(1, chunks, 1, 1, CHUNK, 1)
-    right = right.reshape(levels, chunks, 24, CHUNK * 8)
-    left = left.reshape(levels, chunks, 24, CHUNK * 8)
+    ).reshape(levels, chunks, 24, CHUNK * 8)
+    weight_rows = jnp.repeat(weights, 8).reshape(chunks, 1, CHUNK * 8)
     mix = jnp.transpose(factors.astype(jnp.bfloat16), (0, 3, 2, 4, 1)).reshape(
         levels, 192, terms
     )
+    wide = np.einsum("jqy,lrz->qrjlyz", filters, filters).reshape(64, 256)
+    tall = np.einsum("ipx->ixp", filters).reshape(16, 8)
     counts = [source.shape[0] // 24 for source in sources]
     vmem = pl.BlockSpec(memory_space=pltpu.VMEM)
+    smem = pl.BlockSpec(memory_space=pltpu.SMEM)
     outs = pl.pallas_call(
         apply_kernel,
-        out_shape=tuple(jax.ShapeDtypeStruct((8, n, 64), jnp.float32) for n in counts),
-        in_specs=[vmem] * (3 + levels),
-        out_specs=tuple(vmem for _ in counts),
+        out_shape=tuple(jax.ShapeDtypeStruct((n, 8, 64), jnp.float32) for n in counts[:2]),
+        in_specs=[vmem] * 5 + [smem] * 3 + [vmem] * levels,
+        out_specs=(vmem, vmem),
         scratch_shapes=[pltpu.VMEM((8, n, 8, CHUNK * 64), jnp.float32) for n in counts],
         name="apply_levels",
-    )(left, right, mix, *sources)
-    return [
-        jnp.transpose(out, (1, 0, 2)).reshape(n, 512) for out, n in zip(outs, counts)
-    ]
+    )(
+        right,
+        weight_rows,
+        mix,
+        jnp.asarray(wide),
+        jnp.asarray(tall),
+        live_mask[None, :],
+        child_hot.reshape(-1, child_hot.shape[-1]),
+        octant_hot,
+        *sources,
+    )
+    return tuple(out.reshape(-1, 512) for out in outs)
 
 
 def pick_sources(table, ids):
@@ -313,18 +348,16 @@
     near_slot = jnp.where(mid_nbr >= 0, parent_all[jnp.maximum(mid_nbr, 0)], -1)
     mid_picked = pick_sources(mid_table, near_slot)
     coarse_picked = pick_sources(coarse_table, coarse_nbr[parent])
-    fine_direct, mid_direct, parent_out = apply_levels(
-        op_factor, term_weight, [fine_picked, mid_picked, coarse_picked]
-    )
     octant_hot = (octant[:, None] == jnp.arange(8, dtype=jnp.int32)[None, :]).astype(jnp.float32)
-    mid_out = mid_direct + jnp.sum(
-        octant_hot[:, :, None] * prolong(parent_out, filters), axis=1
-    )
-    fine_back = jnp.einsum(
-        "mos,mok->sk", child_hot, prolong(mid_out, filters), precision=exact_mode
-    )
-    fine_out = live_mask[:, None] * (fine_direct + fine_back)
-    return (fine_out, mid_out)
+    return apply_levels(
+        op_factor,
+        term_weight,
+        [fine_picked, mid_picked, coarse_picked],
+        live_mask,
+        child_hot,
+        octant_hot,
+        filters,
+    )
 
 
 def solution(mesh):

time: 70.8 us -> 67.9 us (0.959)
  matrix products: 14.8 us -> 12.5 us
  local copies, waits for them, and re-layouts: 19 us -> 17.9 us
    dot_general x4 -> x2, matrix products: 6.65 us -> 2.9 us  [prolong(): jnp.einsum('bijxyr,lrz->bijlxyz', section_two, filters, precision=exact_m...]
    pallas_call x2 -> x0, other arithmetic: 2.69 us -> none  [apply_levels(): pl.pallas_call(apply_kernel, out_shape=tuple((jax.ShapeDtypeStruct((8, n,...]
    reshape x4 -> x3, local copies, waits for them, and re-layouts: 2.69 us -> 3.98 us  [the longest x2 2.76 us: apply_levels(): return tuple((out.reshape(-1, 512) for out in outs))]
    gather x6, local copies, waits for them, and re-layouts: 3.75 us -> 2.74 us  [pick_sources(): table[jnp.maximum(ids, 0)] * (ids >= 0)[:, :, None].astype(jnp.bfloat16)]
    dot_general x1 -> x0, matrix products: 0.87 us -> none  [shards(): jnp.einsum('mos,mok->sk', child_hot, prolong(mid_out, filters), precision...]
    broadcast_in_dim x0 -> x3, local copies, waits for them, and re-layouts: none -> 0.84 us  [apply_levels(): weight_rows = jnp.repeat(weights, 8).reshape(chunks, 1, CHUNK * 8)]
    transpose x1 -> x0, local copies, waits for them, and re-layouts: 0.76 us -> none  [apply_levels(): jnp.transpose(out, (1, 0, 2)).reshape(n, 512)]
    mul x2 -> x0, local copies, waits for them, and re-layouts: 0.71 us -> none  [apply_levels(): left = right * weights.reshape(1, chunks, 1, 1, CHUNK, 1)]
where the time goes in v2:
time: 67.9 us; the launch traced here: 67.2 us
  Pallas kernels  29.9 us (44%)
  local copies, waits for them, and re-layouts  17.9 us (26%)
  matrix products  12.5 us (18%)
  other arithmetic  4.42 us (7%)
  between operations  2.42 us (4%)
    pallas_call x1, Pallas kernels, exchange(): pl.pallas_call(lambda *refs: exchange_kernel(sizes, *refs), out_shape=(ja...  16.8 us
    pallas_call x1, Pallas kernels, apply_levels(): pl.pallas_call(apply_kernel, out_shape=tuple((jax.ShapeDtypeStruct((n, 8,...  13.1 us
    dot_general x2, matrix products, prolong(): jnp.einsum('bijxyr,lrz->bijlxyz', section_two, filters, precision=exact_m...  2.9 us
    dot_general x2, matrix products, compress(): jnp.einsum('bijlxyz,ipx->bjlpyz', cube_form, filters, precision=exact_mode)  2.76 us
    reshape x2, local copies, waits for them, and re-layouts, apply_levels(): return tuple((out.reshape(-1, 512) for out in outs))  2.76 us
    gather x6, local copies, waits for them, and re-layouts, pick_sources(): table[jnp.maximum(ids, 0)] * (ids >= 0)[:, :, None].astype(jnp.bfloat16)  2.74 us
    reshape x3, local copies, waits for them, and re-layouts, pick_sources(): return jnp.transpose(picked, (0, 1, 3, 2, 4)).reshape(boxes * 24, 576)  2.55 us
    dot_general x2, matrix products, prolong(): jnp.einsum('bixqr,jqy->bijxyr', section_one, filters, precision=exact_mode)  1.56 us

profile of v2, /device:TPU:0, one launch (start us, length us, event | category | flops | bytes accessed | tf_op | source)
XLA Modules:
  0.0 67.2 jit_solution(8102045365840803844)
XLA Ops:
  2.1 0.7 fusion.45
  2.8 1.3 %gather_fusion = bf16[8,512]{1,0:T(8,128)(2,1)S(1)} fusion(bf16[8,512]{1,0:T(8,128)(2,1)} %param.24, s32[1024]{0:T(1024)S(1)} %pad_clamp_fusion.4), kind=kCustom, calls=%fused_computation | custom fusion | bytes 16416 | tf_op jit(solution)/shard_map/gather | solution.py:317
  4.0 0.2 reshape.364
  4.2 1.0 %convolution_bitcast_fusion.6 = f32[2,2,8,8,8]{4,2,3,1,0:T(8,128)S(1)} fusion(f32[2,8,8,1,1,1]{2,1,0,5,4,3:T(8,128)} %constant.173, bf16[2,2,2,8,8,8]{5,4,3,2,1,0:T(8,128)(2,1)S(1)} %reshape.364), kind=kOutput, calls=%fused_computation.11 | convolution fusion | flops 393216 | bytes 16896 | tf_op jit(solution)/shard_map/bijlxyz,ipx->bjlpyz/dot_general | solution.py:63
  5.2 1.0 %convolution_bitcast_fusion.8 = f32[2,8,8,8]{3,2,1,0:T(8,128)S(1)} fusion(f32[2,8,8,1,1]{2,1,0,4,3:T(8,128)} %constant.172, f32[2,2,8,8,8]{4,2,3,1,0:T(8,128)S(1)} %convolution_bitcast_fusion.6), kind=kOutput, calls=%fused_computation.13 | convolution fusion | flops 196608 | bytes 12800 | tf_op jit(solution)/shard_map/bjlpyz,jqy->blpqz/dot_general | solution.py:64
  6.2 0.9 %convolution_bitcast_fusion.9 = bf16[8,8,8]{2,1,0:T(8,128)(2,1)S(1)} fusion(f32[2,8,8,8]{3,2,1,0:T(8,128)S(1)} %convolution_bitcast_fusion.8, f32[2,8,8,1]{2,1,3,0:T(8,128)} %constant.171), kind=kOutput, calls=%fused_computation.14 | convolution fusion | flops 98304 | bytes 5632 | tf_op jit(solution)/shard_map/blpqz,lrz->bpqr/dot_general | solution.py:65
  7.2 0.7 %fusion.47 = (bf16[512]{0:T(512)(128)(2,1)S(1)}, bf16[1,512]{1,0:T(2,128)(2,1)S(1)}) fusion(bf16[1,512]{1,0:T(2,128)(2,1)S(1)} %reshape.367, bf16[1,512]{1,0:T(2,128)(2,1)} %param.25, pred[]{:T(512)} %bitcast.12), kind=kLoop, calls=%fused_computation.112 | loop fusion | flops 1024 | bytes 4097 | tf_op jit(solution)/shard_map/convert_element_type | solution.py:321
  7.9 0.6 maximum_reduce_fusion
  8.5 0.7 %select_reduce_fusion = f32[8]{0:T(128)S(1)} fusion(f32[]{:T(128)} %bitcast.5, s32[8]{0:T(128)} %bitcast.168), kind=kLoop, calls=%fused_computation.86 | loop fusion | flops 184 | bytes 68 | tf_op jit(solution)/shard_map/reduce_sum | solution.py:316
  9.3 0.9 %fusion.15 = f32[2,8,8,8]{3,1,2,0:T(8,128)S(1)} fusion(f32[2,8,8,1]{2,1,3,0:T(8,128)} %constant.171, bf16[8,8,8]{2,1,0:T(8,128)(2,1)S(1)} %reshape.368), kind=kOutput, calls=%fused_computation.38 | convolution fusion | flops 98304 | bytes 5632 | tf_op jit(solution)/shard_map/bpqr,ipx->bixqr/dot_general | solution.py:73
  10.2 1.0 %convolution_bitcast_fusion.7 = f32[2,2,8,8,8]{4,3,2,0,1:T(8,128)S(1)} fusion(f32[2,8,8,1,1]{2,1,4,3,0:T(8,128)} %constant.170, f32[2,8,8,8]{3,1,2,0:T(8,128)S(1)} %fusion.15), kind=kOutput, calls=%fused_computation.12 | convolution fusion | flops 196608 | bytes 12800 | tf_op jit(solution)/shard_map/bixqr,jqy->bijxyr/dot_general | solution.py:74
  11.3 1.9 %convolution_bitcast_fusion.5 = f32[1,2,2,2,8,8,8]{5,6,4,2,1,3,0:T(8,128)S(1)} fusion(f32[2,8,8,1,1,1]{2,1,5,4,3,0:T(8,128)S(1)} %copy-done.7, f32[2,2,8,8,8]{4,3,2,0,1:T(8,128)S(1)} %convolution_bitcast_fusion.7), kind=kOutput, calls=%fused_computation.10 | convolution fusion | flops 393216 | bytes 25088 | tf_op jit(solution)/shard_map/bijxyr,lrz->bijlxyz/dot_general | solution.py:75
  13.1 0.1 copy.65
  13.3 0.2 reshape.370
  13.4 0.9 %fusion.1.refs_0_ = bf16[8,512]{1,0:T(8,128)(2,1)} fusion(f32[8,512]{1,0:T(8,128)S(1)} %reshape.370, bf16[8,512]{1,0:T(8,128)(2,1)S(1)} %copy-done.2, f32[8]{0:T(128)S(1)} %select_reduce_fusion, s32[8]{0:T(128)S(1)} %bitcast.169), kind=kOutput, calls=%fused_computation.17 | convolution fusion | flops 409664 | bytes 32832 | tf_op jit(solution)/shard_map/mos,mok->sk/dot_general | solution.py:324
  14.3 16.8 %exchange.1 = (bf16[3,3,3,8,512]{4,3,2,1,0:T(8,128)(2,1)}, bf16[4,4,2,1,8,128]{5,4,3,2,1,0:T(8,128)(2,1)}) custom-call(bf16[8,512]{1,0:T(8,128)(2,1)} %fusion.1.refs_0_, bf16[1,8,128]{2,1,0:T(8,128)(2,1)} %bitcast.166), custom_call_target="tpu_custom_call" | custom-call | tf_op jit(solution)/shard_map/exchange/pallas_call | solution.py:165
  31.1 0.9 %copy.139 = bf16[4,8,8,128]{3,1,2,0:T(8,128)(2,1)S(1)} copy(bf16[4,8,8,128]{3,2,1,0:T(8,128)(2,1)} %bitcast.165) | data formatting | bytes 131072
  32.1 0.1 fusion.13
  32.2 0.6 reshape_reshape.7
  32.8 1.8 %convolution_bitcast_fusion.2 = f32[4,2,2,8,8,8]{3,5,4,2,1,0:T(8,128)S(1)} fusion(f32[2,8,8,1,1,1,1]{2,1,0,6,5,4,3:T(8,128)S(1)} %copy-done.4, f32[4,2,2,2,8,8,8]{6,5,4,3,2,1,0:T(8,128)S(1)} %reshape_reshape.7), kind=kOutput, calls=%fused_computation.7 | convolution fusion | flops 1572864 | bytes 98816 | tf_op jit(solution)/shard_map/bijlxyz,ipx->bjlpyz/dot_general | solution.py:63
  34.7 0.5 copy.69
  35.2 0.5 convolution_bitcast_fusion.3
  35.8 0.6 bitcast_convert_fusion
  36.4 0.4 convolution_bitcast_fusion.4
  36.8 0.2 copy.92
  37.0 0.5 convolution_bitcast_fusion.1
  37.6 1.0 %convolution_bitcast_fusion = f32[4,2,2,2,8,8,8]{6,5,3,4,2,1,0:T(8,128)S(1)} fusion(f32[4,2,2,8,8,8,1]{4,5,6,3,2,1,0:T(8,128)S(1)} %convolution_bitcast_fusion.1, f32[2,8,8,1,1,1,1]{2,1,0,6,5,4,3:T(8,128)S(1)} %copy-done.4), kind=kOutput, calls=%fused_computation.5 | convolution fusion | flops 1572864 | bytes 98816 | tf_op jit(solution)/shard_map/bijxyr,lrz->bijlxyz/dot_general | solution.py:75
  38.7 0.5 reshape_reshape.8
  39.3 0.7 %gather_fusion.2 = s32[27]{0:T(128)S(1)} fusion(s32[32]{0:T(128)S(1)} %add_bitcast_fusion, s32[1024]{0:T(1024)S(1)} %pad_clamp_fusion.2), kind=kCustom, calls=%fused_computation.2 | custom fusion | bytes 324 | tf_op jit(solution)/shard_map/gather | solution.py:348
  40.1 0.6 gather_fusion.3
  41.0 0.7 %reshape.375.refs_1_ = bf16[24,576]{1,0:T(8,128)(2,1)} reshape(bf16[1,3,8,9,64]{4,3,2,1,0:T(8,128)(2,1)S(1)} %fusion.10) | data formatting | bytes 55296 | tf_op jit(solution)/shard_map/reshape | solution.py:292
  41.7 0.1 convert_element_type.90
  41.9 0.6 gather_fusion.4
  42.8 0.7 %reshape.376.refs_2_ = bf16[24,576]{1,0:T(8,128)(2,1)} reshape(bf16[1,3,8,9,64]{4,3,2,1,0:T(8,128)(2,1)S(1)} %fusion.9) | data formatting | bytes 55296 | tf_op jit(solution)/shard_map/reshape | solution.py:292
  43.6 1.1 %gather_fusion.1 = bf16[216,512]{1,0:T(8,128)(2,1)S(1)} fusion(bf16[216,512]{1,0:T(8,128)(2,1)S(1)} %bitcast.159, s32[1024]{0:T(1024)S(1)} %pad_clamp_fusion.3), kind=kCustom, calls=%fused_computation.1 | custom fusion | bytes 443232 | tf_op jit(solution)/shard_map/gather | solution.py:290
  44.7 0.2 gather.26
  45.0 0.1 fusion.3
  45.2 1.1 %reshape.373.refs_0_ = bf16[192,576]{1,0:T(8,128)(2,1)} reshape(bf16[8,3,8,9,64]{4,3,2,1,0:T(8,128)(2,1)S(1)} %fusion.3) | data formatting | bytes 442368 | tf_op jit(solution)/shard_map/reshape | solution.py:292
  46.3 0.5 compare_convert_fusion.3.octant_ref
  46.8 0.7 fusion.34.child_ref
  47.4 0.4 copy.54
  47.9 0.6 copy.55
  48.5 1.2 %reshape.362.right_ref = f32[3,8,24,32]{3,2,1,0:T(8,128)} reshape(f32[3,8,3,8,4,8]{5,4,3,2,1,0:T(4,128)S(1)} %copy.55) | data formatting | bytes 147456 | tf_op jit(solution)/shard_map/reshape | solution.py:257
  49.8 0.7 copy.56
  50.6 0.7 %broadcast_in_dim.56.weight_ref = f32[8,1,32]{2,1,0:T(1,128)} reshape(f32[8,4,8]{2,1,0:T(4,128)S(1)} %broadcast_in_dim.55) | data formatting | bytes 2048 | tf_op jit(solution)/shard_map/broadcast_in_dim | solution.py:258
  51.3 13.1 %apply_levels.1 = (f32[8,8,64]{2,1,0:T(8,128)}, f32[1,8,64]{2,1,0:T(8,128)}) custom-call(f32[3,8,24,32]{3,2,1,0:T(8,128)} %reshape.362.right_ref, f32[8,1,32]{2,1,0:T(1,128)} %broadcast_in_dim.56.weight_ref, bf16[3,192,32]{2,1,0:T(8,128)(2,1)} %bitcast.161, f32[64,256]{1,0:T(8,128)} %constant.139.clone.wide_ref, f32[16,8]{1,0:T(8,128)} %constant.140.clone.tall_ref, ...), custom_call_target="tpu_custom_call" | custom-call | tf_op jit(solution)/shard_map/apply_levels/pallas_call | solution.py:267
  64.4 1.4 %reshape.377 = f32[8,512]{1,0:T(8,128)} reshape(f32[8,8,64]{2,1,0:T(8,128)} %get-tuple-element.8) | data formatting | bytes 32768 | tf_op jit(solution)/shard_map/reshape | solution.py:285
  65.8 1.3 %reshape.378 = f32[1,512]{1,0:T(1,128)} reshape(f32[1,8,64]{2,1,0:T(8,128)} %get-tuple-element.9) | data formatting | bytes 4096 | tf_op jit(solution)/shard_map/reshape | solution.py:285
  (59 shorter events, 1.6 us)
Async XLA Ops:
  0.6 10.6 %copy-start.7 = (f32[2,8,8,1,1,1]{2,1,5,4,3,0:T(8,128)S(1)}, f32[2,8,8,1,1,1]{2,1,5,4,3,0:T(8,128)}, u32[]{:S(2)}) copy-start(f32[2,8,8,1,1,1]{2,1,5,4,3,0:T(8,128)} %constant.169) | copy-start | bytes 1540
  1.3 12.1 %copy-start.2 = (bf16[8,512]{1,0:T(8,128)(2,1)S(1)}, bf16[8,512]{1,0:T(8,128)(2,1)}, u32[]{:S(2)}) copy-start(bf16[8,512]{1,0:T(8,128)(2,1)} %param.24) | copy-start | bytes 24580
  1.4 12.1 %copy-start.10 = (s32[1,8]{1,0:T(1,128)S(1)}, s32[1,8]{1,0:T(1,128)}, u32[]{:S(2)}) copy-start(s32[1,8]{1,0:T(1,128)} %param.26) | copy-start | bytes 100
  9.2 23.6 %copy-start.9 = (f32[8]{0:T(128)}, f32[8]{0:T(128)S(1)}, u32[]{:S(2)}) copy-start(f32[8]{0:T(128)S(1)} %select_reduce_fusion) | copy-start | bytes 100
  13.1 19.7 %copy-start.4 = (f32[2,8,8,1,1,1,1]{2,1,0,6,5,4,3:T(8,128)S(1)}, f32[2,8,8,1,1,1,1]{2,1,0,6,5,4,3:T(8,128)}, u32[]{:S(2)}) copy-start(f32[2,8,8,1,1,1,1]{2,1,0,6,5,4,3:T(8,128)} %constant.174) | copy-start | bytes 1540
  32.8 2.4 %copy-start.6 = (f32[2,8,8,1,1,1]{2,1,0,4,5,3:T(8,128)S(1)}, f32[2,8,8,1,1,1]{2,1,0,4,5,3:T(8,128)}, u32[]{:S(2)}) copy-start(f32[2,8,8,1,1,1]{2,1,0,4,5,3:T(8,128)} %constant.175) | copy-start | bytes 1540
  34.7 1.1 %copy-start.3 = (f32[2,8,8,1,1]{2,1,0,4,3:T(8,128)S(1)}, f32[2,8,8,1,1]{2,1,0,4,3:T(8,128)}, u32[]{:S(2)}) copy-start(f32[2,8,8,1,1]{2,1,0,4,3:T(8,128)} %constant.172) | copy-start | bytes 1540
  35.2 1.8 %copy-start.5 = (f32[2,8,8,1,1,1]{2,1,5,0,4,3:T(8,128)S(1)}, f32[2,8,8,1,1,1]{2,1,5,0,4,3:T(8,128)}, u32[]{:S(2)}) copy-start(f32[2,8,8,1,1,1]{2,1,5,0,4,3:T(8,128)} %constant.176) | copy-start | bytes 1540
  38.6 0.7 %copy-start.12 = (s32[1,27]{1,0:T(1,128)S(1)}, s32[1,27]{1,0:T(1,128)}, u32[]{:S(2)}) copy-start(s32[1,27]{1,0:T(1,128)} %param.30) | copy-start | bytes 328
  38.7 2.0 %copy-start.13 = (s32[4,27]{1,0:T(4,128)S(1)}, s32[4,27]{1,0:T(4,128)}, u32[]{:S(2)}) copy-start(s32[4,27]{1,0:T(4,128)} %param.31) | copy-start | bytes 1300
  39.3 4.2 %copy-start.8 = (s32[8,27]{1,0:T(8,128)S(1)}, s32[8,27]{1,0:T(8,128)}, u32[]{:S(2)}) copy-start(s32[8,27]{1,0:T(8,128)} %param.29) | copy-start | bytes 2596
  39.3 4.4 %copy-start = (bf16[3,3,3,8,512]{4,3,2,1,0:T(8,128)(2,1)S(1)}, bf16[3,3,3,8,512]{4,3,2,1,0:T(8,128)(2,1)}, u32[]{:S(2)}) copy-start(bf16[3,3,3,8,512]{4,3,2,1,0:T(8,128)(2,1)} %get-tuple-element.6) | copy-start | bytes 663556
  44.9 2.5 %copy-start.1 = (f32[3,32,3,8,8]{1,4,3,2,0:T(8,128)S(1)}, f32[3,32,3,8,8]{1,4,3,2,0:T(8,128)}, u32[]{:S(2)}) copy-start(f32[3,32,3,8,8]{1,4,3,2,0:T(8,128)} %param.32) | copy-start | bytes 221188
  48.5 1.9 %copy-start.11 = (f32[32]{0:T(128)S(1)}, f32[32]{0:T(128)}, u32[]{:S(2)}) copy-start(f32[32]{0:T(128)} %param.33) | copy-start | bytes 388
